TPU v7x, 32 devices: a whole 2x2x4 slice. The times are simulated.
32 devices in a mesh: tm: 2 (over x), lat: 4 (over y, core), lon: 4 (over z).
Axes of the slice: x: 2, y: 2, z: 4, core: 2. Of those that a mesh axis runs over, the one named last changes fastest.
Arguments:
- control: float32 [16, 8, 64, 512], P(None, None, 'lat', 'lon'), may hold values from -6 to 6
- ens_pert: bfloat16 [2, 16, 8, 64, 512], P('tm', None, None, 'lat', 'lon'), may hold values from -6 to 6
- lat_filter: bfloat16 [64, 64], replicated, may hold values from 0 to 2.5, as said below
- lon_filter: bfloat16 [512, 512], replicated, may hold values from 0 to 2.5, as said below
- interp_lat: float32 [128, 18], P('lat'), may hold values from -1.5 to 1.5
- interp_lon: float32 [1024, 130], P('lon'), may hold values from -0.5 to 0.5
- obs_cell: int32 [2, 2, 4, 4, 64], P('tm', None, 'lat', 'lon'), may hold values from 0 to 65535
- obs_count: int32 [2, 2, 4, 4], P('tm', None, 'lat', 'lon'), may hold values from 1 to 64, as said below
- obs_value: float32 [2, 2, 4, 4, 64], P('tm', None, 'lat', 'lon'), may hold values from -18 to 18
- obs_weight: float32 [2, 2, 4, 4, 64], P('tm', None, 'lat', 'lon'), may hold values from 0.1 to 0.4
Outputs:
- gradient: float32 [16, 8, 64, 512], P(None, None, 'lat', 'lon')
Inputs may be any that keep to these rules, and one draw needn't show every extreme that they name: `lat_filter`: within the latitude spreading matrix all entries are non-negative. `lon_filter`: entries are non-negative. `obs_count`: each count is at least 1 and at most 64; in every draw some count equals 64.
All inputs are finite; a program needn't handle non-finite values.
Results may differ from a plain program's by a relative error of at most 0.0003.
Values sent between devices are 32-bit elements; how exact they have to be, the bound alone decides.
No kernel may reach another device: no remote copies, remote signals or barrier semaphores. Data moves between devices by JAX's collectives and lax.ppermute only.
A program may use at most 64 MiB of HBM per device.

v0:
```python
import functools
import math

import jax
import jax.numpy as jnp
from jax import lax
from jax.experimental import pallas as pl
from jax.experimental.pallas import tpu as pltpu
from jax.sharding import PartitionSpec as P


HIGHEST = lax.Precision.HIGHEST
F32 = jnp.float32
BF16 = jnp.bfloat16


def swap(x, axis, k):
    return lax.ppermute(x, axis, [(i, i ^ k) for i in range(lax.axis_size(axis))])


def split(x):
    high = x.astype(BF16)
    return high, (x - high.astype(F32)).astype(BF16)


def dot(x, y, dims=((1,), (0,)), precision=None):
    return lax.dot_general(
        x, y, (dims, ((), ())), precision=precision, preferred_element_type=F32
    )


def vmem_call(kernel, out_shape, operands, flops, scratch=(), smem=0):
    specs = [pl.BlockSpec(memory_space=pltpu.SMEM)] * smem
    specs += [pl.BlockSpec(memory_space=pltpu.VMEM)] * (len(operands) - smem)
    nbytes = sum(math.prod(x.shape) * x.dtype.itemsize for x in [*operands, *out_shape])
    return pl.pallas_call(
        kernel,
        out_shape=out_shape,
        in_specs=specs,
        out_specs=[pl.BlockSpec(memory_space=pltpu.VMEM)] * len(out_shape),
        scratch_shapes=list(scratch),
        cost_estimate=pl.CostEstimate(flops=flops, bytes_accessed=nbytes, transcendentals=0),
        compiler_params=pltpu.CompilerParams(vmem_limit_bytes=2 * nbytes + 2**22),
    )(*operands)


def struct(*shape):
    return jax.ShapeDtypeStruct(shape, F32)


def cut_kernel(bands, slots, share, group, *refs):
    pert, outs, first, last = refs[0], refs[1:-2], refs[-2], refs[-1]
    rows, width = pert.shape[4:]
    t, b = lax.axis_index("tm"), lax.axis_index("lon")
    held = pert.shape[2]
    for q in range(slots):
        member = lax.div(t ^ q, held) * share
        level = lax.rem(t ^ q, held)
        for k in range(bands):
            for inner in range(group):
                part = pert[pl.ds(member, share), b ^ k, level, inner]
                part = part.astype(F32)
                at = inner * share * rows
                outs[q * bands + k][at : at + share * rows, :] = part.reshape(share * rows, width)
                at = ((q * bands + k) * group + inner) * share
                first[at : at + share, :] = part[:, 0, :]
                last[at : at + share, :] = part[:, rows - 1, :]


def weight_kernel(lats, rows, repeat, matrix, ahead, back):
    a = lax.axis_index("lat")
    length = matrix.shape[1]
    size = repeat * rows
    full = size + 2 * repeat
    iota = lax.broadcasted_iota

    def pick(shape, axis, wanted):
        return jnp.where(iota(jnp.int32, shape, axis) == wanted, 1.0, 0.0).astype(BF16)

    def block(to, of):
        line = iota(jnp.int32, (full, length), 0)
        rim = line - size
        wanted = jnp.where(
            rim < 0,
            to * rows + jnp.bitwise_and(line, rows - 1),
            to * rows + jnp.where(rim < repeat, -1, rows),
        )
        chosen = dot(pick((full, length), 1, wanted), matrix[...]).astype(BF16)
        column = iota(jnp.int32, (length, size), 1)
        chosen = dot(chosen, pick((length, size), 0, of * rows + jnp.bitwise_and(column, rows - 1)))
        line, column = iota(jnp.int32, (full, size), 0), iota(jnp.int32, (full, size), 1)
        rim = line - size
        field = jnp.where(rim < 0, line // rows, jnp.bitwise_and(rim, repeat - 1))
        return jnp.where(field == column // rows, chosen, 0.0)

    for h in range(0, lats, 2):
        at = h // 2 * full
        wide = jnp.concatenate([block(a ^ h, a ^ j) for j in (0, 1)], axis=1)
        ahead[at : at + full, :] = jnp.concatenate([wide, wide], axis=1).astype(BF16)
        at = h // 2 * size
        wide = jnp.concatenate([block(a ^ j, a ^ h).T for j in (0, 1)], axis=1)
        back[at : at + size, :] = jnp.concatenate([wide, wide], axis=1).astype(BF16)


def package_kernel(slots, count, cell, value, weight, *outs):
    t = lax.axis_index("tm")
    cap = cell.shape[1]
    entry = lax.broadcasted_iota(jnp.int32, (1, cap), 1)
    for q in range(slots):
        slot = t ^ q
        at = pl.ds(slot, 1)
        usable = jnp.where(entry < count[slot], 1.0, 0.0)
        lines = [cell[at, :].astype(F32), value[at, :], weight[at, :] * usable]
        outs[q][...] = jnp.concatenate(lines + [jnp.zeros((5, cap), F32)], axis=0)


def list_kernel(slots, held, half, *refs):
    package, interp, outs, turned = refs[:slots], refs[slots], refs[slots + 1 : -1], refs[-1]
    count, cap = interp.shape[0], package[0].shape[1]
    cols = interp.shape[1] // held
    part = lax.rem(lax.axis_index("tm"), held)
    mine = interp[:, :cols]
    for n in range(1, held):
        mine = jnp.where(part == n, interp[:, n * cols : (n + 1) * cols], mine)
    turned[...] = jnp.concatenate(
        [
            mine[1 : count - 1],
            mine[:1],
            mine[count - 1 :],
            jnp.zeros((turned.shape[0] - count, cols), F32),
        ],
        axis=0,
    )
    start = jnp.bitwise_and(lax.axis_index("lat"), 1) * (turned.shape[0] - half)
    outs[0][:half, :] = turned[pl.ds(pl.multiple_of(start, 8), half), :]
    at = outs[-1].shape[0] - 8
    for h in range(slots):
        outs[-1][at:, h * cap : (h + 1) * cap] = package[h][...]


def merge_kernel(bands, fields, *refs):
    rims, parts, outs = refs[:fields], refs[fields:-bands], refs[-bands:]
    edge = rims[0].shape[1]
    tall = outs[0].shape[0] - len(rims) * edge
    b = lax.axis_index("lon")
    for k in range(bands):
        at = pl.ds(pl.multiple_of((b ^ k) * tall, 8), tall)
        total = parts[0][at, :]
        for part in parts[1:]:
            total = total + part[at, :]
        outs[k][:tall, :] = total
        for q, rim in enumerate(rims):
            outs[k][tall + q * edge : tall + (q + 1) * edge, :] = rim[k]


def gather_kernel(*refs):
    out = refs[-1]
    for k, ref in enumerate(refs[:-1]):
        out[k] = ref[: out.shape[1], :]


def finish_kernel(bands, slots, share, group, control, *refs):
    pieces, out = refs[:-1], refs[-1]
    rows, width = control.shape[4:]
    t, b = lax.axis_index("tm"), lax.axis_index("lon")
    held = control.shape[2]
    for q in range(slots):
        member = pl.ds(lax.div(t ^ q, held) * share, share)
        level = lax.rem(t ^ q, held)
        for k in range(bands):
            for inner in range(group):
                at = inner * share * rows
                part = pieces[q * bands + k][at : at + share * rows, :].reshape(share, rows, width)
                old = control[member, b ^ k, level, inner]
                out[member, b ^ k, level, inner] = old + part


def pairs(blocks):
    return [
        blocks[i] if i + 1 == len(blocks) else jnp.concatenate(blocks[i : i + 2], axis=1)
        for i in range(0, len(blocks), 2)
    ]


def lat_kernel(share, group, rows, repeat, own, other, weights, *outs):
    table = weights[...]
    size, width = repeat * rows, own.shape[1]
    full = size + 2 * repeat
    fields = group * share * rows
    tall = fields + 2 * group * share
    blocks = []
    for i in range(own.shape[0] // size):
        block = jnp.concatenate([ref[i * size : (i + 1) * size, :] for ref in (own, other)], axis=0)
        blocks.append(block)
    for pair, block in enumerate(pairs(blocks)):
        result = dot(table, jnp.concatenate(split(block), axis=0))
        for side in range(block.shape[1] // width):
            line = (2 * pair + side) * repeat
            band, inner, member = line // (group * share), line // share % group, line % share
            at = band * tall + (inner * share + member) * rows
            span = slice(side * width, (side + 1) * width)
            for h, out in enumerate(outs):
                base = h * full
                out[at : at + size, :] = result[base : base + size, span]
                for rim in (0, 1):
                    to = band * tall + fields + (2 * inner + rim) * share + member
                    of = base + size + rim * repeat
                    out[to : to + repeat, :] = result[of : of + repeat, span]


def lat_back_kernel(bands, share, group, rows, repeat, own, other, weights, *outs):
    table = weights[...]
    size, width = repeat * rows, own.shape[1]
    fields = group * share * rows
    tall = fields + 2 * group * share
    blocks, where = [], []
    for k in range(bands):
        for inner in range(group):
            for member in range(0, share, repeat):
                block = []
                for ref in (own, other):
                    at = k * tall + (inner * share + member) * rows
                    block.append(ref[at : at + size, :])
                    for rim in (0, 1):
                        at = k * tall + fields + (2 * inner + rim) * share + member
                        block.append(ref[at : at + repeat, :])
                blocks.append(jnp.concatenate(block, axis=0))
                where.append((k, (inner * share + member) * rows))
    for pair, block in enumerate(pairs(blocks)):
        result = dot(table, jnp.concatenate(split(block), axis=0))
        for side in range(block.shape[1] // width):
            k, at = where[2 * pair + side]
            span = slice(side * width, (side + 1) * width)
            for h in range(len(outs) // bands):
                outs[h * bands + k][at : at + size, :] = result[h * size : (h + 1) * size, span]


def increment_stage(sizes, source, table, pert, rims, window):
    bands, slots, share, group, rows, padded, width = sizes
    fields = group * share * rows
    pieces = [split(f[: fields + 2 * group * share, :]) for f in source]
    high, low = (jnp.concatenate([p[i] for p in pieces], axis=1) for i in (0, 1))
    part = table[...]
    spread = dot(high, part) + dot(low, part)
    filler = jnp.zeros((padded - rows - 2, width), F32)
    for q in range(slots):
        for k in range(bands):
            span = slice(k * width, (k + 1) * width)
            for inner in range(group):
                total = None
                for m in range(share):
                    at = (inner * share + m) * rows
                    term = spread[at : at + rows, span] * pert[q * bands + k][at : at + rows, :]
                    total = term if total is None else total + term
                block = [total]
                for rim in (0, 1):
                    at = (2 * inner + rim) * share
                    at_edge = rims[k].shape[0] + (q - slots) * 2 * group * share + at
                    edge = rims[k][at_edge : at_edge + share, :]
                    edge = spread[fields + at : fields + at + share, span] * edge
                    block.append(jnp.sum(edge, axis=0, keepdims=True))
                at = (q * group + inner) * padded
                window[k, at : at + padded, :] = jnp.concatenate(block + [filler], axis=0)


def observe_stage(sizes, window, tables, grad):
    bands, _, _, _, _, _, width = sizes
    onto, back, chosen, ends = tables
    tall = chosen.shape[1]
    lane = lax.broadcasted_iota(jnp.int32, (tall, width), 1)
    b = lax.axis_index("lon")
    for k in range(bands):
        grad[k] = jnp.zeros((tall, width), F32)
    for k in range(bands):
        before = b ^ lax.rem((b ^ k) + bands - 1, bands)
        after = b ^ lax.rem((b ^ k) + 1, bands)
        upper, lower = split(window[k])
        table = onto[k]
        left, right = ends[k, 0:1], ends[k, 1:2]
        seen_by = dot(jnp.concatenate([upper, upper], axis=1), table) + dot(lower, table[:width])
        seen_by += window[before][:, width - 1 : width] * left
        seen_by += window[after][:, 0:1] * right
        pick = chosen[k]
        seen = jnp.sum(pick * seen_by, axis=0, keepdims=True)
        weighted = pick * (ends[k, 4:5] * (seen - ends[k, 3:4]))
        upper, lower = split(weighted)
        table = back[k]
        both = dot(upper, table)
        grad[k] += both[:, :width] + both[:, width:] + dot(lower, table[:, :width])
        onto_left = jnp.sum(weighted * left, axis=1, keepdims=True)
        onto_right = jnp.sum(weighted * right, axis=1, keepdims=True)
        grad[before] += jnp.where(lane == width - 1, onto_left, 0.0)
        grad[after] += jnp.where(lane == 0, onto_right, 0.0)


def adjoint_stage(sizes, grads, table, pert, rims, outs):
    bands, slots, share, group, rows, padded, width = sizes
    held = slots // len(grads)
    fields = group * share * rows
    columns = []
    for k in range(bands):
        pieces = []
        for inner in range(group):
            lines = [
                grads[q // held][k, pl.ds((q % held * group + inner) * padded, padded), :]
                for q in range(slots)
            ]
            for m in range(share):
                at = (inner * share + m) * rows
                pieces.append(sum(
                    lines[q][:rows] * pert[q * bands + k][at : at + rows, :] for q in range(slots)
                ))
        for inner in range(group):
            for rim in (0, 1):
                at = (2 * inner + rim) * share
                total = 0.0
                for q in range(slots):
                    line = (q % held * group + inner) * padded + rows + rim
                    line = grads[q // held][k, line : line + 1, :]
                    edge = rims[k].shape[0] + (q - slots) * 2 * group * share + at
                    total += line * rims[k][edge : edge + share, :]
                pieces.append(total)
        columns.append(split(jnp.concatenate(pieces, axis=0)))
    high, low = (jnp.concatenate([c[i] for c in columns], axis=1) for i in (0, 1))
    part = table[...]
    result = dot(high, part) + dot(low, part)
    tall = fields + 2 * group * share
    for k in range(bands):
        out, at = (outs[1], 0) if len(outs) > 1 and k == bands - 1 else (outs[0], k * tall)
        out[at : at + tall, :] = result[:, k * width : (k + 1) * width]


def middle_kernel(sizes, *refs):
    bands, slots = sizes[:2]
    source, turned, table, rest = refs[:bands], refs[bands], refs[bands + 1], refs[bands + 2 :]
    pert, rims, rest = rest[: slots * bands], source, rest[slots * bands :]
    tables, outs, (window, grad) = rest[:4], rest[4:-2], rest[-2:]
    increment_stage(sizes, source, turned, pert, rims, window)
    observe_stage(sizes, window, tables, grad)
    adjoint_stage(sizes, [grad], table, pert, rims, outs)


def increment_kernel(sizes, *refs):
    bands = sizes[0]
    pert, out = refs[bands + 1 : -1], refs[-1]
    increment_stage(sizes, refs[:bands], refs[bands], pert, refs[:bands], out)


def observe_kernel(sizes, window, onto, back, chosen, ends, grad):
    observe_stage(sizes, window, (onto, back, chosen, ends), grad)


def adjoint_kernel(sizes, sets, *refs):
    bands, slots = sizes[:2]
    grads, table, rest = refs[:sets], refs[sets], refs[sets + 1 :]
    pert, rest = rest[: bands * slots], rest[bands * slots :]
    adjoint_stage(sizes, grads, table, pert, rest[:bands], rest[bands:])


def prepare_kernel(sizes, held, half, fine, *refs):
    bands, _, _, levels, rows, padded, width = sizes
    parts, packs, interp_lat = refs[: 2 * held], refs[2 * held : 3 * held], refs[3 * held]
    onto, back, chosen, ends, full = refs[3 * held + 1 :]
    fine_rows, fine_cols = fine
    count = packs[0].shape[2]
    obs = held * count
    cols = fine_cols // held
    tm = lax.rem(lax.axis_index("tm"), held)
    first = ((lax.axis_index("lon") * held + tm) * levels).astype(F32)
    parity = jnp.bitwise_and(lax.axis_index("lat"), 1)
    lat = interp_lat[...]
    lat = jnp.concatenate(
        [lat[1 : rows + 1], lat[:1], lat[rows + 1 :], jnp.zeros((padded - rows - 2, fine_rows), F32)], axis=0
    )
    slot = lax.broadcasted_iota(jnp.int32, (1, obs), 1) // count
    for k in range(bands):
        base = packs[0].shape[1] - 8
        lines = jnp.concatenate([pack[k, base:, :] for pack in packs], axis=1)
        cell = lines[0:1] + 0.5
        level = jnp.floor(cell * (1.0 / (fine_rows * fine_cols)))
        inside = cell - level * (fine_rows * fine_cols)
        row = jnp.floor(inside * (1.0 / fine_cols))
        col = jnp.floor(inside - row * fine_cols).astype(jnp.int32)
        line = lax.broadcasted_iota(jnp.int32, (cols, obs), 0)
        hot = [
            jnp.where(line == col - jnp.bitwise_xor(tm, j) * cols, 1.0, 0.0).astype(BF16)
            for j in range(held)
        ]
        hot = jnp.concatenate(hot, axis=0)
        for side in (0, 1):
            part = jnp.concatenate([parts[2 * j + side][k, :half, :] for j in range(held)], axis=1)
            upper, lower = split(part)
            start = jnp.bitwise_xor(parity, side) * (full.shape[0] - half)
            full[pl.ds(pl.multiple_of(start, 8), half), :] = dot(upper, hot) + dot(lower, hot)
        main = full[:width, :]
        upper, lower = split(main)
        onto[k, :width, :] = upper
        onto[k, width:, :] = lower
        upper, lower = split(main.T)
        back[k, :, :width] = upper
        back[k, :, width:] = lower
        line = lax.broadcasted_iota(jnp.int32, (fine_rows, obs), 0)
        hot = jnp.where(line == row.astype(jnp.int32), 1.0, 0.0)
        rowpart = dot(lat, hot, precision=HIGHEST)
        ends[k] = jnp.concatenate([full[width : width + 2, :], level, lines[1:3], lines[3:6]], axis=0)
        for j in range(held):
            for inner in range(levels):
                at = (j * levels + inner) * padded
                fits = jnp.logical_and(level == first + inner, slot == j)
                chosen[k, at : at + padded, :] = jnp.where(fits, rowpart, 0.0)


def per_device(
    control,
    ens_pert,
    lat_filter,
    lon_filter,
    interp_lat,
    interp_lon,
    obs_cell,
    obs_count,
    obs_value,
    obs_weight,
):
    slots, lats, lons = (lax.axis_size(axis) for axis in ("tm", "lat", "lon"))
    t, _, b = (lax.axis_index(axis) for axis in ("tm", "lat", "lon"))
    members, levels, rows, width = control.shape
    held = math.gcd(slots, levels // lons)
    parts = slots // held
    share = members // parts
    group = levels // (lons * held)
    fields = group * share * rows
    edge = 2 * group * share
    tall = fields + edge
    whole = lons * width
    padded = -(-(rows + 2) // 8) * 8
    sizes = (lons, slots, share, group, rows, padded, width)
    split_up = (members, lons, held, group, rows, width)
    by_group = control.reshape(split_up)

    repeat = math.gcd(share, max(64 // rows, 1))

    size = repeat * rows
    full = size + 2 * repeat
    ahead, weights = vmem_call(
        functools.partial(weight_kernel, lats, rows, repeat),
        [
            jax.ShapeDtypeStruct((lats // 2 * full, 4 * size), BF16),
            jax.ShapeDtypeStruct((lats // 2 * size, 4 * full), BF16),
        ],
        [lat_filter],
        0,
    )

    count = slots * lons
    cut = vmem_call(
        functools.partial(cut_kernel, lons, slots, share, group),
        [struct(fields, width)] * count + [struct(count * group * share, width)] * 2,
        [ens_pert[0].reshape(split_up)],
        0,
    )
    pert = [None] * count
    order = [*range(2, lons), *range(1, min(lons, 2)), 0]
    for k in order:
        for q in range(slots):
            piece = cut[q * lons + k]
            if q > 0:
                piece = swap(piece, "tm", q)
            pert[q * lons + k] = piece if k == 0 else swap(piece, "lon", k)
    up = [(i, i + 1) for i in range(lats - 1)]
    down = [(i + 1, i) for i in range(lats - 1)]

    mine = lax.dynamic_slice(
        by_group,
        (t // held * share, 0, t % held, 0, 0, 0),
        (share, lons, 1, group, rows, width),
    )
    mine = jnp.transpose(mine, (1, 2, 3, 0, 4, 5)).reshape(lons * fields, width)
    mixed = vmem_call(
        functools.partial(lat_kernel, share, group, rows, repeat),
        [struct(lons * tall, width)] * (lats // 2),
        [mine, swap(mine, "lat", 1), ahead],
        2 * ahead.shape[0] * 4 * mine.size,
    )
    arrived = [swap(mixed[h], "lat", 2 * h) for h in range(1, lats // 2)]

    rim = cut[-2:]
    before = lax.ppermute(rim[1], "lat", up).reshape(slots, lons, group, 1, share, width)
    after = lax.ppermute(rim[0], "lat", down).reshape(slots, lons, group, 1, share, width)
    rim = jnp.concatenate([before, after], axis=3).reshape(slots, lons, edge, width)
    rims = [rim[0]] + [swap(rim[q], "tm", q) for q in range(1, slots)]

    cap = obs_cell.shape[-1]
    package = vmem_call(
        functools.partial(package_kernel, slots),
        [struct(8, cap)] * slots,
        [obs_count.reshape(slots)] + [x.reshape(slots, cap) for x in (obs_cell, obs_value, obs_weight)],
        0,
        smem=1,
    )
    package = [package[0]] + [swap(package[q], "tm", q) for q in range(1, slots)]
    entries = slots * cap
    fine = interp_lat.shape[0], interp_lon.shape[0]
    cols = fine[1] // held
    turned_rows = -(-(width + 2) // 8) * 8
    half = -(-turned_rows // 16) * 8
    fuse = entries == cols
    shapes = [struct(half + 8, cols)] if fuse else [struct(half, cols), struct(8, entries)]
    listing = vmem_call(
        functools.partial(list_kernel, slots, held, half),
        shapes,
        [*package, interp_lon.T],
        0,
        scratch=[pltpu.VMEM((turned_rows, cols), F32)],
    )
    near = [[x] + [swap(x, "lon", k) for k in range(1, lons)] for x in listing]
    source = vmem_call(
        functools.partial(merge_kernel, lons, slots),
        [struct(tall + slots * edge, width)] * lons,
        [*rims, mixed[0], *arrived],
        0,
    )
    source = [source[0]] + [swap(source[k], "lon", k) for k in range(1, lons)]
    near = [vmem_call(gather_kernel, [struct(lons, *x[0].shape)], x, 0)[0] for x in near]
    slices, packs = [], []
    for j in range(held):
        here = near if j == 0 else [swap(x, "tm", j) for x in near]
        slices += [here[0], swap(here[0], "lat", 1)]
        packs.append(here[-1])
    window_rows = held * group * padded
    obs = held * entries
    lists = vmem_call(
        functools.partial(prepare_kernel, sizes, held, half, fine),
        [
            jax.ShapeDtypeStruct((lons, 2 * width, obs), BF16),
            jax.ShapeDtypeStruct((lons, obs, 2 * width), BF16),
            struct(lons, window_rows, obs),
            struct(lons, 8, obs),
        ],
        [*slices, *packs, interp_lat.T],
        8 * lons * obs * width * fine[1],
        scratch=[pltpu.VMEM((turned_rows, obs), F32)],
    )

    tall_table = jnp.concatenate(
        [lax.dynamic_slice_in_dim(lon_filter, (b ^ k) * width, width, 0) for k in range(lons)], axis=0
    )
    table = jnp.concatenate(
        [lax.dynamic_slice_in_dim(tall_table, (b ^ k) * width, width, 1) for k in range(lons)], axis=1
    )
    turned = table.T
    flops = 4 * tall * whole * whole
    scratch = [pltpu.VMEM((lons, window_rows, width), F32)] * 2
    early = max(lons - 1, 1)
    shapes = [struct(early * tall, width)] + [struct(tall, width)] * (lons - early)
    if parts == 1:
        spread = vmem_call(
            functools.partial(middle_kernel, sizes),
            shapes,
            [*source, turned, table, *pert, *lists],
            2 * flops,
            scratch=scratch,
        )
    else:
        [every] = vmem_call(
            functools.partial(increment_kernel, sizes),
            [struct(lons, slots * group * padded, width)],
            [*source, turned, *pert],
            flops,
        )
        window = every[:, :window_rows]
        for h in range(1, parts):
            window += swap(every[:, h * window_rows :][:, :window_rows], "tm", h * held)
        [grad] = vmem_call(
            functools.partial(observe_kernel, sizes),
            [struct(lons, window_rows, width)],
            [window, *lists],
            8 * window_rows * whole * obs,
        )
        grads = [grad] + [swap(grad, "tm", h * held) for h in range(1, parts)]
        spread = vmem_call(
            functools.partial(adjoint_kernel, sizes, parts), shapes, [*grads, table, *pert, *source], flops
        )

    def lat_back(x, count):
        out = vmem_call(
            functools.partial(lat_back_kernel, count, share, group, rows, repeat),
            [struct(fields, width)] * (count * (lats // 2)),
            [x, swap(x, "lat", 1), weights],
            8 * weights.shape[0] * x.size,
        )
        pieces = []
        for n in range(count):
            piece = out[n]
            for h in range(1, lats // 2):
                piece = piece + swap(out[h * count + n], "lat", 2 * h)
            pieces.append(piece)
        return pieces

    done = {}
    for k, piece in enumerate(lat_back(spread[0], early)):
        done[k] = swap(piece, "lon", k) if k > 0 else piece
    if early < lons:
        piece = swap(spread[1], "lon", early)
        [done[early]] = lat_back(piece, 1)
    arrived = {}
    for k in done:
        arrived[k, 0] = done[k]
        for q in range(1, slots):
            arrived[k, q] = swap(done[k], "tm", q)
    pieces = [arrived[k, q] for q in range(slots) for k in range(lons)]
    [result] = vmem_call(
        functools.partial(finish_kernel, lons, slots, share, group),
        [struct(*split_up)],
        [by_group, *pieces],
        control.size,
    )
    return result.reshape(control.shape)


def solution(mesh):
    placed = (
        P(None, None, "lat", "lon"),
        P("tm", None, None, "lat", "lon"),
        P(),
        P(),
        P("lat", None),
        P("lon", None),
        P("tm", None, "lat", "lon", None),
        P("tm", None, "lat", "lon"),
        P("tm", None, "lat", "lon", None),
        P("tm", None, "lat", "lon", None),
    )
    return jax.shard_map(
        per_device,
        mesh=mesh,
        in_specs=placed,
        out_specs=P(None, None, "lat", "lon"),
        check_vma=False,
    )
```

profile of v0, /device:TPU:0, one launch (start us, length us, event | category | flops | bytes accessed | tf_op | source)
XLA Modules:
  0.0 117.5 jit_solution(11491815010455082146)
XLA Ops:
  4.4 2.9 %collective-permute-start.4 = (f32[1152,128]{1,0:T(8,128)}, f32[1152,128]{1,0:T(8,128)S(1)}, u32[]{:S(2)}, u32[]{:S(2)}) collective-permute-start(f32[1152,128]{1,0:T(8,128)} %get-tuple-element.43), channel_id=1, source_target_pairs={{0,8},{4,12},{8,0},{12,4},{1,9},{5,13},{9,1},{13,5},{2,10},{6,14},... | collective-permute-start | bytes 1769480 | tf_op jit(solution)/shard_map/ppermute | solution.py:18
  8.7 3.0 %collective-permute-start = (f32[128,128]{1,0:T(8,128)S(1)}, f32[128,128]{1,0:T(8,128)S(1)}, u32[]{:S(2)}, u32[]{:S(2)}) collective-permute-start(f32[128,128]{1,0:T(8,128)S(1)} %get-tuple-element.39), channel_id=1, source_target_pairs={{0,4},{4,8},{8,12},{1,5},{5,9},{9,13},{2,6},{6,10},{10,14},{3,7},{... | collective-permute-start | bytes 196616 | tf_op jit(solution)/shard_map/ppermute | solution.py:488
  18.4 2.6 %collective-permute-start.20 = (f32[80,128]{1,0:T(8,128)S(1)}, f32[80,128]{1,0:T(8,128)S(1)}, u32[]{:S(2)}, u32[]{:S(2)}) collective-permute-start(f32[80,128]{1,0:T(8,128)S(1)} %shard_map.105.refs_0_), channel_id=1, source_target_pairs={{0,2},{1,3},{2,0},{3,1},{4,6},{5,7},{6,4},{7,5},{8,10},{9,11},{10,... | collective-permute-start | bytes 122888 | tf_op jit(solution)/shard_map/ppermute | solution.py:18
  22.5 2.7 %collective-permute-start.21 = (f32[80,128]{1,0:T(8,128)S(1)}, f32[80,128]{1,0:T(8,128)S(1)}, u32[]{:S(2)}, u32[]{:S(2)}) collective-permute-start(f32[80,128]{1,0:T(8,128)S(1)} %shard_map.105.refs_0_), channel_id=1, source_target_pairs={{0,3},{1,2},{2,1},{3,0},{4,7},{5,6},{6,5},{7,4},{8,11},{9,10},{10,... | collective-permute-start | bytes 122888 | tf_op jit(solution)/shard_map/ppermute | solution.py:18
  25.8 2.5 %collective-permute-done.21.refs_3_ = f32[80,128]{1,0:T(8,128)S(1)} collective-permute-done((f32[80,128]{1,0:T(8,128)S(1)}, f32[80,128]{1,0:T(8,128)S(1)}, u32[]{:S(2)}, u32[]{:S(2)}) %collective-permute-start.21) | collective-permute-done | bytes 40992 | tf_op jit(solution)/shard_map/ppermute | solution.py:18
  28.3 2.8 %collective-permute-start.10 = (f32[256,128]{1,0:T(8,128)S(1)}, f32[256,128]{1,0:T(8,128)S(1)}, u32[]{:S(2)}, u32[]{:S(2)}) collective-permute-start(f32[256,128]{1,0:T(8,128)S(1)} %get-tuple-element.51), channel_id=1, source_target_pairs={{0,3},{1,2},{2,1},{3,0},{4,7},{5,6},{6,5},{7,4},{8,11},{9,10},{10,... | collective-permute-start | bytes 393224 | tf_op jit(solution)/shard_map/ppermute | solution.py:18
  33.2 4.4 %collective-permute-done.9.refs_8_ = f32[256,128]{1,0:T(8,128)S(1)} collective-permute-done((f32[256,128]{1,0:T(8,128)S(1)}, f32[256,128]{1,0:T(8,128)S(1)}, u32[]{:S(2)}, u32[]{:S(2)}) %collective-permute-start.9) | collective-permute-done | bytes 131104 | tf_op jit(solution)/shard_map/ppermute | solution.py:18
  41.4 3.3 %collective-permute-done.23.refs_2_.refs_5_ = f32[4,80,128]{2,1,0:T(8,128)S(1)} collective-permute-done((f32[4,80,128]{2,1,0:T(8,128)S(1)}, f32[4,80,128]{2,1,0:T(8,128)S(1)}, u32[]{:S(2)}, u32[]{:S(2)}) %collective-permute-start.23) | collective-permute-done | bytes 163872 | tf_op jit(solution)/shard_map/ppermute | solution.py:18
  45.6 2.0 %collective-permute-done.14 = f32[256,128]{1,0:T(8,128)} collective-permute-done((f32[256,128]{1,0:T(8,128)S(1)}, f32[256,128]{1,0:T(8,128)}, u32[]{:S(2)}, u32[]{:S(2)}) %collective-permute-start.14) | collective-permute-done | bytes 131104 | tf_op jit(solution)/shard_map/ppermute | solution.py:18
  47.6 2.4 %collective-permute-done.16 = f32[256,128]{1,0:T(8,128)} collective-permute-done((f32[256,128]{1,0:T(8,128)S(1)}, f32[256,128]{1,0:T(8,128)}, u32[]{:S(2)}, u32[]{:S(2)}) %collective-permute-start.16) | collective-permute-done | bytes 131104 | tf_op jit(solution)/shard_map/ppermute | solution.py:18
  52.3 2.1 %collective-permute-start.15 = (f32[256,128]{1,0:T(8,128)}, f32[256,128]{1,0:T(8,128)S(1)}, u32[]{:S(2)}, u32[]{:S(2)}) collective-permute-start(f32[256,128]{1,0:T(8,128)} %collective-permute-done.14), channel_id=1, source_target_pairs={{0,2},{1,3},{2,0},{3,1},{4,6},{5,7},{6,4},{7,5},{8,10},{9,11},{10,... | collective-permute-start | bytes 393224 | tf_op jit(solution)/shard_map/ppermute | solution.py:18
  54.4 1.7 %collective-permute-start.17 = (f32[256,128]{1,0:T(8,128)}, f32[256,128]{1,0:T(8,128)}, u32[]{:S(2)}, u32[]{:S(2)}) collective-permute-start(f32[256,128]{1,0:T(8,128)} %collective-permute-done.16), channel_id=1, source_target_pairs={{0,3},{1,2},{2,1},{3,0},{4,7},{5,6},{6,5},{7,4},{8,11},{9,10},{10,... | collective-permute-start | bytes 393224 | tf_op jit(solution)/shard_map/ppermute | solution.py:18
  59.0 19.6 %collective-permute-done.15.refs_12_ = f32[256,128]{1,0:T(8,128)S(1)} collective-permute-done((f32[256,128]{1,0:T(8,128)}, f32[256,128]{1,0:T(8,128)S(1)}, u32[]{:S(2)}, u32[]{:S(2)}) %collective-permute-start.15) | collective-permute-done | bytes 131104 | tf_op jit(solution)/shard_map/ppermute | solution.py:18
  78.6 2.5 %shard_map.108 = (f32[864,128]{1,0:T(8,128)S(1)}, f32[288,128]{1,0:T(8,128)S(1)}) custom-call(f32[352,128]{1,0:T(8,128)S(1)} %get-tuple-element.44.refs_0_, f32[352,128]{1,0:T(8,128)S(1)} %collective-permute-done.5.refs_1_, f32[352,128]{1,0:T(8,128)S(1)} %collective-permute-done.6.refs_2_, f32[352,128]{1,0:T(8,128)S(1)} %collective-permute-done.7.refs_3_, ...), custom_call_target="tpu_custom_call" | custom-call | flops 603979776 | bytes 4685824 | tf_op jit(solution)/shard_map/pallas_call | solution.py:36
  81.3 1.8 %collective-permute-start.31 = (f32[288,128]{1,0:T(8,128)S(1)}, f32[288,128]{1,0:T(8,128)S(1)}, u32[]{:S(2)}, u32[]{:S(2)}) collective-permute-start(f32[288,128]{1,0:T(8,128)S(1)} %get-tuple-element.70), channel_id=1, source_target_pairs={{0,3},{1,2},{2,1},{3,0},{4,7},{5,6},{6,5},{7,4},{8,11},{9,10},{10,... | collective-permute-start | bytes 442376 | tf_op jit(solution)/shard_map/ppermute | solution.py:18
  83.1 6.3 %collective-permute-done.31.own = f32[288,128]{1,0:T(8,128)S(1)} collective-permute-done((f32[288,128]{1,0:T(8,128)S(1)}, f32[288,128]{1,0:T(8,128)S(1)}, u32[]{:S(2)}, u32[]{:S(2)}) %collective-permute-start.31) | collective-permute-done | bytes 147488 | tf_op jit(solution)/shard_map/ppermute | solution.py:18
  89.9 2.0 %collective-permute-start.29 = (f32[256,128]{1,0:T(8,128)S(1)}, f32[256,128]{1,0:T(8,128)S(1)}, u32[]{:S(2)}, u32[]{:S(2)}) collective-permute-start(f32[256,128]{1,0:T(8,128)S(1)} %get-tuple-element.69), channel_id=1, source_target_pairs={{0,8},{4,12},{8,0},{12,4},{1,9},{5,13},{9,1},{13,5},{2,10},{6,14},... | collective-permute-start | bytes 393224 | tf_op jit(solution)/shard_map/ppermute | solution.py:18
  92.3 1.9 %collective-permute-start.26 = (f32[256,128]{1,0:T(8,128)S(1)}, f32[256,128]{1,0:T(8,128)S(1)}, u32[]{:S(2)}, u32[]{:S(2)}) collective-permute-start(f32[256,128]{1,0:T(8,128)S(1)} %get-tuple-element.65), channel_id=1, source_target_pairs={{0,8},{4,12},{8,0},{12,4},{1,9},{5,13},{9,1},{13,5},{2,10},{6,14},... | collective-permute-start | bytes 393224 | tf_op jit(solution)/shard_map/ppermute | solution.py:18
  94.2 2.0 %collective-permute-done.27 = f32[256,128]{1,0:T(8,128)S(1)} collective-permute-done((f32[256,128]{1,0:T(8,128)S(1)}, f32[256,128]{1,0:T(8,128)S(1)}, u32[]{:S(2)}, u32[]{:S(2)}) %collective-permute-start.27) | collective-permute-done | bytes 131104 | tf_op jit(solution)/shard_map/ppermute | solution.py:18
  96.3 3.7 %collective-permute-start.28 = (f32[256,128]{1,0:T(8,128)S(1)}, f32[256,128]{1,0:T(8,128)S(1)}, u32[]{:S(2)}, u32[]{:S(2)}) collective-permute-start(f32[256,128]{1,0:T(8,128)S(1)} %add.44), channel_id=1, source_target_pairs={{0,1},{1,0},{2,3},{3,2},{4,5},{5,4},{6,7},{7,6},{8,9},{9,8},{10,11... | collective-permute-start | bytes 393224 | tf_op jit(solution)/shard_map/ppermute | solution.py:18
  99.9 3.2 %collective-permute-start.30 = (f32[256,128]{1,0:T(8,128)S(1)}, f32[256,128]{1,0:T(8,128)S(1)}, u32[]{:S(2)}, u32[]{:S(2)}) collective-permute-start(f32[256,128]{1,0:T(8,128)S(1)} %add.45), channel_id=1, source_target_pairs={{0,2},{1,3},{2,0},{3,1},{4,6},{5,7},{6,4},{7,5},{8,10},{9,11},{10,... | collective-permute-start | bytes 393224 | tf_op jit(solution)/shard_map/ppermute | solution.py:18
  106.3 2.6 %collective-permute-done.30.refs_2_ = f32[256,128]{1,0:T(8,128)S(1)} collective-permute-done((f32[256,128]{1,0:T(8,128)S(1)}, f32[256,128]{1,0:T(8,128)S(1)}, u32[]{:S(2)}, u32[]{:S(2)}) %collective-permute-start.30) | collective-permute-done | bytes 131104 | tf_op jit(solution)/shard_map/ppermute | solution.py:18
  109.6 2.8 %collective-permute-done.34.refs_4_ = f32[256,128]{1,0:T(8,128)S(1)} collective-permute-done((f32[256,128]{1,0:T(8,128)S(1)}, f32[256,128]{1,0:T(8,128)S(1)}, u32[]{:S(2)}, u32[]{:S(2)}) %collective-permute-start.34) | collective-permute-done | bytes 131104 | tf_op jit(solution)/shard_map/ppermute | solution.py:18
  112.4 2.6 %collective-permute-done.35.refs_5_ = f32[256,128]{1,0:T(8,128)S(1)} collective-permute-done((f32[256,128]{1,0:T(8,128)S(1)}, f32[256,128]{1,0:T(8,128)S(1)}, u32[]{:S(2)}, u32[]{:S(2)}) %collective-permute-start.35) | collective-permute-done | bytes 131104 | tf_op jit(solution)/shard_map/ppermute | solution.py:18
  (94 shorter events, 33.8 us)
Async XLA Ops:
  4.4 40.3 %collective-permute-start.4 = (f32[1152,128]{1,0:T(8,128)}, f32[1152,128]{1,0:T(8,128)S(1)}, u32[]{:S(2)}, u32[]{:S(2)}) collective-permute-start(f32[1152,128]{1,0:T(8,128)} %get-tuple-element.43), channel_id=1, source_target_pairs={{0,8},{4,12},{8,0},{12,4},{1,9},{5,13},{9,1},{13,5},{2,10},{6,14},... | collective-permute-start | bytes 1769480 | tf_op jit(solution)/shard_map/ppermute | solution.py:18
  7.4 10.9 %collective-permute-start.1 = (f32[128,128]{1,0:T(8,128)S(1)}, f32[128,128]{1,0:T(8,128)S(1)}, u32[]{:S(2)}, u32[]{:S(2)}) collective-permute-start(f32[128,128]{1,0:T(8,128)S(1)} %get-tuple-element.40), channel_id=1, source_target_pairs={{4,0},{8,4},{12,8},{5,1},{9,5},{13,9},{6,2},{10,6},{14,10},{7,3},{... | collective-permute-start | bytes 196616 | tf_op jit(solution)/shard_map/ppermute | solution.py:489
  8.7 12.2 %collective-permute-start = (f32[128,128]{1,0:T(8,128)S(1)}, f32[128,128]{1,0:T(8,128)S(1)}, u32[]{:S(2)}, u32[]{:S(2)}) collective-permute-start(f32[128,128]{1,0:T(8,128)S(1)} %get-tuple-element.39), channel_id=1, source_target_pairs={{0,4},{4,8},{8,12},{1,5},{5,9},{9,13},{2,6},{6,10},{10,14},{3,7},{... | collective-permute-start | bytes 196616 | tf_op jit(solution)/shard_map/ppermute | solution.py:488
  14.6 17.2 %collective-permute-start.8 = (f32[256,128]{1,0:T(8,128)S(1)}, f32[256,128]{1,0:T(8,128)S(1)}, u32[]{:S(2)}, u32[]{:S(2)}) collective-permute-start(f32[256,128]{1,0:T(8,128)S(1)} %get-tuple-element.49), channel_id=1, source_target_pairs={{0,1},{1,0},{2,3},{3,2},{4,5},{5,4},{6,7},{7,6},{8,9},{9,8},{10,11... | collective-permute-start | bytes 393224 | tf_op jit(solution)/shard_map/ppermute | solution.py:18
  21.0 10.2 %collective-permute-start.2 = (f32[4,32,128]{2,1,0:T(8,128)S(1)}, f32[4,32,128]{2,1,0:T(8,128)S(1)}, u32[]{:S(2)}, u32[]{:S(2)}) collective-permute-start(f32[4,32,128]{2,1,0:T(8,128)S(1)} %bitcast.36), channel_id=1, source_target_pairs={{0,16},{16,0},{1,17},{17,1},{2,18},{18,2},{3,19},{19,3},{4,20},{20... | collective-permute-start | bytes 196616 | tf_op jit(solution)/shard_map/ppermute | solution.py:18
  25.3 12.3 %collective-permute-start.9 = (f32[256,128]{1,0:T(8,128)S(1)}, f32[256,128]{1,0:T(8,128)S(1)}, u32[]{:S(2)}, u32[]{:S(2)}) collective-permute-start(f32[256,128]{1,0:T(8,128)S(1)} %get-tuple-element.50), channel_id=1, source_target_pairs={{0,2},{1,3},{2,0},{3,1},{4,6},{5,7},{6,4},{7,5},{8,10},{9,11},{10,... | collective-permute-start | bytes 393224 | tf_op jit(solution)/shard_map/ppermute | solution.py:18
  28.3 9.9 %collective-permute-start.10 = (f32[256,128]{1,0:T(8,128)S(1)}, f32[256,128]{1,0:T(8,128)S(1)}, u32[]{:S(2)}, u32[]{:S(2)}) collective-permute-start(f32[256,128]{1,0:T(8,128)S(1)} %get-tuple-element.51), channel_id=1, source_target_pairs={{0,3},{1,2},{2,1},{3,0},{4,7},{5,6},{6,5},{7,4},{8,11},{9,10},{10,... | collective-permute-start | bytes 393224 | tf_op jit(solution)/shard_map/ppermute | solution.py:18
  31.2 8.5 %collective-permute-start.11 = (f32[256,128]{1,0:T(8,128)S(1)}, f32[256,128]{1,0:T(8,128)S(1)}, u32[]{:S(2)}, u32[]{:S(2)}) collective-permute-start(f32[256,128]{1,0:T(8,128)S(1)} %get-tuple-element.52), channel_id=1, source_target_pairs={{0,16},{16,0},{1,17},{17,1},{2,18},{18,2},{3,19},{19,3},{4,20},{20... | collective-permute-start | bytes 393224 | tf_op jit(solution)/shard_map/ppermute | solution.py:18
  31.8 8.5 %collective-permute-start.12 = (f32[256,128]{1,0:T(8,128)S(1)}, f32[256,128]{1,0:T(8,128)S(1)}, u32[]{:S(2)}, u32[]{:S(2)}) collective-permute-start(f32[256,128]{1,0:T(8,128)S(1)} %get-tuple-element.53), channel_id=1, source_target_pairs={{0,16},{16,0},{1,17},{17,1},{2,18},{18,2},{3,19},{19,3},{4,20},{20... | collective-permute-start | bytes 393224 | tf_op jit(solution)/shard_map/ppermute | solution.py:18
  38.2 9.4 %collective-permute-start.14 = (f32[256,128]{1,0:T(8,128)S(1)}, f32[256,128]{1,0:T(8,128)}, u32[]{:S(2)}, u32[]{:S(2)}) collective-permute-start(f32[256,128]{1,0:T(8,128)S(1)} %get-tuple-element.54), channel_id=1, source_target_pairs={{0,16},{16,0},{1,17},{17,1},{2,18},{18,2},{3,19},{19,3},{4,20},{20... | collective-permute-start | bytes 393224 | tf_op jit(solution)/shard_map/ppermute | solution.py:18
  39.6 10.4 %collective-permute-start.16 = (f32[256,128]{1,0:T(8,128)S(1)}, f32[256,128]{1,0:T(8,128)}, u32[]{:S(2)}, u32[]{:S(2)}) collective-permute-start(f32[256,128]{1,0:T(8,128)S(1)} %get-tuple-element.55), channel_id=1, source_target_pairs={{0,16},{16,0},{1,17},{17,1},{2,18},{18,2},{3,19},{19,3},{4,20},{20... | collective-permute-start | bytes 393224 | tf_op jit(solution)/shard_map/ppermute | solution.py:18
  40.3 10.4 %collective-permute-start.22 = (f32[4,80,128]{2,1,0:T(8,128)S(1)}, f32[4,80,128]{2,1,0:T(8,128)S(1)}, u32[]{:S(2)}, u32[]{:S(2)}) collective-permute-start(f32[4,80,128]{2,1,0:T(8,128)S(1)} %shard_map.106.refs_0_.refs_4_), channel_id=1, source_target_pairs={{0,4},{4,0},{8,12},{12,8},{1,5},{5,1},{9,13},{13,9},{2,6},{6,2},{1... | collective-permute-start | bytes 491528 | tf_op jit(solution)/shard_map/ppermute | solution.py:18
  44.7 9.7 %collective-permute-start.24 = (f32[4,80,128]{2,1,0:T(8,128)S(1)}, f32[4,80,128]{2,1,0:T(8,128)S(1)}, u32[]{:S(2)}, u32[]{:S(2)}) collective-permute-start(f32[4,80,128]{2,1,0:T(8,128)S(1)} %collective-permute-done.23.refs_2_.refs_5_), channel_id=1, source_target_pairs={{0,4},{4,0},{8,12},{12,8},{1,5},{5,1},{9,13},{13,9},{2,6},{6,2},{1... | collective-permute-start | bytes 491528 | tf_op jit(solution)/shard_map/ppermute | solution.py:18
  47.6 31.0 %collective-permute-start.5 = (f32[352,128]{1,0:T(8,128)}, f32[352,128]{1,0:T(8,128)S(1)}, u32[]{:S(2)}, u32[]{:S(2)}) collective-permute-start(f32[352,128]{1,0:T(8,128)} %get-tuple-element.45), channel_id=1, source_target_pairs={{0,1},{1,0},{2,3},{3,2},{4,5},{5,4},{6,7},{7,6},{8,9},{9,8},{10,11... | collective-permute-start | bytes 540680 | tf_op jit(solution)/shard_map/ppermute | solution.py:18
  50.1 28.5 %collective-permute-start.6 = (f32[352,128]{1,0:T(8,128)}, f32[352,128]{1,0:T(8,128)S(1)}, u32[]{:S(2)}, u32[]{:S(2)}) collective-permute-start(f32[352,128]{1,0:T(8,128)} %get-tuple-element.46), channel_id=1, source_target_pairs={{0,2},{1,3},{2,0},{3,1},{4,6},{5,7},{6,4},{7,5},{8,10},{9,11},{10,... | collective-permute-start | bytes 540680 | tf_op jit(solution)/shard_map/ppermute | solution.py:18
  50.6 28.0 %collective-permute-start.7 = (f32[352,128]{1,0:T(8,128)}, f32[352,128]{1,0:T(8,128)S(1)}, u32[]{:S(2)}, u32[]{:S(2)}) collective-permute-start(f32[352,128]{1,0:T(8,128)} %get-tuple-element.47), channel_id=1, source_target_pairs={{0,3},{1,2},{2,1},{3,0},{4,7},{5,6},{6,5},{7,4},{8,11},{9,10},{10,... | collective-permute-start | bytes 540680 | tf_op jit(solution)/shard_map/ppermute | solution.py:18
  52.3 26.3 %collective-permute-start.15 = (f32[256,128]{1,0:T(8,128)}, f32[256,128]{1,0:T(8,128)S(1)}, u32[]{:S(2)}, u32[]{:S(2)}) collective-permute-start(f32[256,128]{1,0:T(8,128)} %collective-permute-done.14), channel_id=1, source_target_pairs={{0,2},{1,3},{2,0},{3,1},{4,6},{5,7},{6,4},{7,5},{8,10},{9,11},{10,... | collective-permute-start | bytes 393224 | tf_op jit(solution)/shard_map/ppermute | solution.py:18
  54.4 24.2 %collective-permute-start.17 = (f32[256,128]{1,0:T(8,128)}, f32[256,128]{1,0:T(8,128)}, u32[]{:S(2)}, u32[]{:S(2)}) collective-permute-start(f32[256,128]{1,0:T(8,128)} %collective-permute-done.16), channel_id=1, source_target_pairs={{0,3},{1,2},{2,1},{3,0},{4,7},{5,6},{6,5},{7,4},{8,11},{9,10},{10,... | collective-permute-start | bytes 393224 | tf_op jit(solution)/shard_map/ppermute | solution.py:18
  89.9 10.0 %collective-permute-start.29 = (f32[256,128]{1,0:T(8,128)S(1)}, f32[256,128]{1,0:T(8,128)S(1)}, u32[]{:S(2)}, u32[]{:S(2)}) collective-permute-start(f32[256,128]{1,0:T(8,128)S(1)} %get-tuple-element.69), channel_id=1, source_target_pairs={{0,8},{4,12},{8,0},{12,4},{1,9},{5,13},{9,1},{13,5},{2,10},{6,14},... | collective-permute-start | bytes 393224 | tf_op jit(solution)/shard_map/ppermute | solution.py:18
  92.1 11.0 %collective-permute-start.33 = (f32[256,128]{1,0:T(8,128)S(1)}, f32[256,128]{1,0:T(8,128)S(1)}, u32[]{:S(2)}, u32[]{:S(2)}) collective-permute-start(f32[256,128]{1,0:T(8,128)S(1)} %get-tuple-element.72), channel_id=1, source_target_pairs={{0,8},{4,12},{8,0},{12,4},{1,9},{5,13},{9,1},{13,5},{2,10},{6,14},... | collective-permute-start | bytes 393224 | tf_op jit(solution)/shard_map/ppermute | solution.py:18
  92.3 11.9 %collective-permute-start.26 = (f32[256,128]{1,0:T(8,128)S(1)}, f32[256,128]{1,0:T(8,128)S(1)}, u32[]{:S(2)}, u32[]{:S(2)}) collective-permute-start(f32[256,128]{1,0:T(8,128)S(1)} %get-tuple-element.65), channel_id=1, source_target_pairs={{0,8},{4,12},{8,0},{12,4},{1,9},{5,13},{9,1},{13,5},{2,10},{6,14},... | collective-permute-start | bytes 393224 | tf_op jit(solution)/shard_map/ppermute | solution.py:18
  96.3 9.1 %collective-permute-start.28 = (f32[256,128]{1,0:T(8,128)S(1)}, f32[256,128]{1,0:T(8,128)S(1)}, u32[]{:S(2)}, u32[]{:S(2)}) collective-permute-start(f32[256,128]{1,0:T(8,128)S(1)} %add.44), channel_id=1, source_target_pairs={{0,1},{1,0},{2,3},{3,2},{4,5},{5,4},{6,7},{7,6},{8,9},{9,8},{10,11... | collective-permute-start | bytes 393224 | tf_op jit(solution)/shard_map/ppermute | solution.py:18
  99.9 8.9 %collective-permute-start.30 = (f32[256,128]{1,0:T(8,128)S(1)}, f32[256,128]{1,0:T(8,128)S(1)}, u32[]{:S(2)}, u32[]{:S(2)}) collective-permute-start(f32[256,128]{1,0:T(8,128)S(1)} %add.45), channel_id=1, source_target_pairs={{0,2},{1,3},{2,0},{3,1},{4,6},{5,7},{6,4},{7,5},{8,10},{9,11},{10,... | collective-permute-start | bytes 393224 | tf_op jit(solution)/shard_map/ppermute | solution.py:18
  105.3 9.6 %collective-permute-start.35 = (f32[256,128]{1,0:T(8,128)S(1)}, f32[256,128]{1,0:T(8,128)S(1)}, u32[]{:S(2)}, u32[]{:S(2)}) collective-permute-start(f32[256,128]{1,0:T(8,128)S(1)} %collective-permute-done.28.refs_1_), channel_id=1, source_target_pairs={{0,16},{16,0},{1,17},{17,1},{2,18},{18,2},{3,19},{19,3},{4,20},{20... | collective-permute-start | bytes 393224 | tf_op jit(solution)/shard_map/ppermute | solution.py:18
  (23 other events, 138.7 us)
where the time goes:
time: 118 us; the launch traced here: 117 us
  waiting for transfers between devices  53.4 us (45%)
  starting transfers between devices  49.9 us (42%)
  Pallas kernels  8.59 us (7%)
  local copies, waits for them, and re-layouts  4.39 us (4%)
    ppermute x36, waiting for transfers between devices, swap(): lax.ppermute(x, axis, [(i, i ^ k) for i in range(lax.axis_size(axis))])  53.4 us
    ppermute x36, starting transfers between devices, swap(): lax.ppermute(x, axis, [(i, i ^ k) for i in range(lax.axis_size(axis))])  45.5 us
    pallas_call x12, Pallas kernels, vmem_call(): pl.pallas_call(kernel, out_shape=out_shape, in_specs=specs, out_specs=[pl...  8.59 us
    ppermute x1, starting transfers between devices, per_device(): lax.ppermute(rim[1], 'lat', up).reshape(slots, lons, group, 1, share, width)  3.03 us
  transfers between devices with their start and end apart: 38, of which 15 were waited for; matrix products, arithmetic and copies ran while one was open for 3% of the time, Pallas kernels for 3%

commit v1 on v0

--- a/solution.py
+++ b/solution.py
@@ -173,6 +173,18 @@
                 part = pieces[q * bands + k][at : at + share * rows, :].reshape(share, rows, width)
                 old = control[member, b ^ k, level, inner]
                 out[member, b ^ k, level, inner] = old + part
+
+
+def spin_kernel(bands, matrix, table, turned):
+    b = lax.axis_index("lon")
+    width = matrix.shape[0] // bands
+    for k in range(bands):
+        at = pl.ds(pl.multiple_of((b ^ k) * width, width), width)
+        for j in range(bands):
+            block = matrix[at, pl.ds(pl.multiple_of((b ^ j) * width, width), width)]
+            ks, js = slice(k * width, (k + 1) * width), slice(j * width, (j + 1) * width)
+            table[ks, js] = block
+            turned[js, ks] = block.astype(F32).T.astype(BF16)
 
 
 def pairs(blocks):
@@ -423,7 +435,7 @@
     obs_weight,
 ):
     slots, lats, lons = (lax.axis_size(axis) for axis in ("tm", "lat", "lon"))
-    t, _, b = (lax.axis_index(axis) for axis in ("tm", "lat", "lon"))
+    t, a, _ = (lax.axis_index(axis) for axis in ("tm", "lat", "lon"))
     members, levels, rows, width = control.shape
     held = math.gcd(slots, levels // lons)
     parts = slots // held
@@ -467,9 +479,6 @@
             if q > 0:
                 piece = swap(piece, "tm", q)
             pert[q * lons + k] = piece if k == 0 else swap(piece, "lon", k)
-    up = [(i, i + 1) for i in range(lats - 1)]
-    down = [(i + 1, i) for i in range(lats - 1)]
-
     mine = lax.dynamic_slice(
         by_group,
         (t // held * share, 0, t % held, 0, 0, 0),
@@ -485,8 +494,14 @@
     arrived = [swap(mixed[h], "lat", 2 * h) for h in range(1, lats // 2)]
 
     rim = cut[-2:]
-    before = lax.ppermute(rim[1], "lat", up).reshape(slots, lons, group, 1, share, width)
-    after = lax.ppermute(rim[0], "lat", down).reshape(slots, lons, group, 1, share, width)
+    odd = jnp.bitwise_and(a, 1) == 1
+    inside = swap(jnp.where(odd, rim[0], rim[1]), "lat", 1)
+    across = [(i, i + 1) for i in range(1, lats - 1, 2)]
+    across += [(j, i) for i, j in across]
+    outside = lax.ppermute(jnp.where(odd, rim[1], rim[0]), "lat", across)
+    form = (slots, lons, group, 1, share, width)
+    before = jnp.where(odd, inside, outside).reshape(form)
+    after = jnp.where(odd, outside, inside).reshape(form)
     rim = jnp.concatenate([before, after], axis=3).reshape(slots, lons, edge, width)
     rims = [rim[0]] + [swap(rim[q], "tm", q) for q in range(1, slots)]
 
@@ -542,13 +557,12 @@
         scratch=[pltpu.VMEM((turned_rows, obs), F32)],
     )
 
-    tall_table = jnp.concatenate(
-        [lax.dynamic_slice_in_dim(lon_filter, (b ^ k) * width, width, 0) for k in range(lons)], axis=0
-    )
-    table = jnp.concatenate(
-        [lax.dynamic_slice_in_dim(tall_table, (b ^ k) * width, width, 1) for k in range(lons)], axis=1
-    )
-    turned = table.T
+    table, turned = vmem_call(
+        functools.partial(spin_kernel, lons),
+        [jax.ShapeDtypeStruct((whole, whole), BF16)] * 2,
+        [lon_filter],
+        0,
+    )
     flops = 4 * tall * whole * whole
     scratch = [pltpu.VMEM((lons, window_rows, width), F32)] * 2
     early = max(lons - 1, 1)
@@ -579,7 +593,10 @@
         )
         grads = [grad] + [swap(grad, "tm", h * held) for h in range(1, parts)]
         spread = vmem_call(
-            functools.partial(adjoint_kernel, sizes, parts), shapes, [*grads, table, *pert, *source], flops
+            functools.partial(adjoint_kernel, sizes, parts),
+            shapes,
+            [*grads, table, *pert, *source],
+            flops,
         )
 
     def lat_back(x, count):

time: 118 us -> 107 us (0.907)
  starting transfers between devices: 49.9 us -> 43.3 us
  local copies, waits for them, and re-layouts: 4.39 us -> 1.61 us
  Pallas kernels: 8.59 us -> 6.27 us
  waiting for transfers between devices: 53.4 us -> 54.7 us
    ppermute x2 -> x1, starting transfers between devices: 4.33 us -> 0.65 us  [per_device(): outside = lax.ppermute(jnp.where(odd, rim[1], rim[0]), 'lat', across)]
    ppermute x36 -> x37, starting transfers between devices: 45.5 us -> 42.6 us  [swap(): lax.ppermute(x, axis, [(i, i ^ k) for i in range(lax.axis_size(axis))])]
    pallas_call x12 -> x13, Pallas kernels: 8.59 us -> 6.27 us  [vmem_call(): pl.pallas_call(kernel, out_shape=out_shape, in_specs=specs, out_specs=[pl...]
    ppermute x36 -> x37, waiting for transfers between devices: 53.4 us -> 54.7 us  [swap(): lax.ppermute(x, axis, [(i, i ^ k) for i in range(lax.axis_size(axis))])]
    transpose x1 -> x0, local copies, waits for them, and re-layouts: 1.27 us -> none  [per_device(): turned = table.T]
    dynamic_slice x2 -> x0, local copies, waits for them, and re-layouts: 1.22 us -> none  [the longest x1 1.13 us: per_device(): lax.dynamic_slice_in_dim(lon_filter, (b ^ k) * width, width, 0)]
  transfers between devices with their start and end apart: 38 -> 38, of which waited for: 15 -> 16; matrix products, arithmetic and copies ran while one was open for 3% -> 0% of each run, Pallas kernels for 3% -> 3%
where the time goes in v1:
time: 107 us; the launch traced here: 106 us
  waiting for transfers between devices  54.7 us (51%)
  starting transfers between devices  43.3 us (40%)
  Pallas kernels  6.27 us (6%)
  local copies, waits for them, and re-layouts  1.61 us (2%)
    ppermute x37, waiting for transfers between devices, swap(): lax.ppermute(x, axis, [(i, i ^ k) for i in range(lax.axis_size(axis))])  54.7 us
    ppermute x37, starting transfers between devices, swap(): lax.ppermute(x, axis, [(i, i ^ k) for i in range(lax.axis_size(axis))])  42.6 us
    pallas_call x13, Pallas kernels, vmem_call(): pl.pallas_call(kernel, out_shape=out_shape, in_specs=specs, out_specs=[pl...  6.27 us
  transfers between devices with their start and end apart: 38, of which 16 were waited for; matrix products, arithmetic and copies ran while one was open for 0% of the time, Pallas kernels for 3%

profile of v1, /device:TPU:0, one launch (start us, length us, event | category | flops | bytes accessed | tf_op | source)
XLA Modules:
  0.0 106.3 jit_solution(2528960100164358888)
XLA Ops:
  4.2 2.6 %collective-permute-start.18 = (f32[8,64]{1,0:T(8,128)S(1)}, f32[8,64]{1,0:T(8,128)S(1)}, u32[]{:S(2)}, u32[]{:S(2)}) collective-permute-start(f32[8,64]{1,0:T(8,128)S(1)} %get-tuple-element.61), channel_id=1, source_target_pairs={{0,16},{16,0},{1,17},{17,1},{2,18},{18,2},{3,19},{19,3},{4,20},{20... | collective-permute-start | bytes 6152 | tf_op jit(solution)/shard_map/ppermute | solution.py:18
  8.3 2.0 %collective-permute-start.14 = (f32[256,128]{1,0:T(8,128)S(1)}, f32[256,128]{1,0:T(8,128)S(1)}, u32[]{:S(2)}, u32[]{:S(2)}) collective-permute-start(f32[256,128]{1,0:T(8,128)S(1)} %get-tuple-element.58), channel_id=1, source_target_pairs={{0,16},{16,0},{1,17},{17,1},{2,18},{18,2},{3,19},{19,3},{4,20},{20... | collective-permute-start | bytes 393224 | tf_op jit(solution)/shard_map/ppermute | solution.py:18
  10.4 1.6 %collective-permute-start.19 = (f32[80,128]{1,0:T(8,128)S(1)}, f32[80,128]{1,0:T(8,128)S(1)}, u32[]{:S(2)}, u32[]{:S(2)}) collective-permute-start(f32[80,128]{1,0:T(8,128)S(1)} %shard_map.106.refs_0_), channel_id=1, source_target_pairs={{0,1},{1,0},{2,3},{3,2},{4,5},{5,4},{6,7},{7,6},{8,9},{9,8},{10,11... | collective-permute-start | bytes 122888 | tf_op jit(solution)/shard_map/ppermute | solution.py:18
  12.4 2.6 %collective-permute-start.20 = (f32[80,128]{1,0:T(8,128)S(1)}, f32[80,128]{1,0:T(8,128)S(1)}, u32[]{:S(2)}, u32[]{:S(2)}) collective-permute-start(f32[80,128]{1,0:T(8,128)S(1)} %shard_map.106.refs_0_), channel_id=1, source_target_pairs={{0,2},{1,3},{2,0},{3,1},{4,6},{5,7},{6,4},{7,5},{8,10},{9,11},{10,... | collective-permute-start | bytes 122888 | tf_op jit(solution)/shard_map/ppermute | solution.py:18
  15.0 3.4 %collective-permute-start.4 = (f32[1152,128]{1,0:T(8,128)S(1)}, f32[1152,128]{1,0:T(8,128)S(1)}, u32[]{:S(2)}, u32[]{:S(2)}) collective-permute-start(f32[1152,128]{1,0:T(8,128)S(1)} %get-tuple-element.45), channel_id=1, source_target_pairs={{0,8},{4,12},{8,0},{12,4},{1,9},{5,13},{9,1},{13,5},{2,10},{6,14},... | collective-permute-start | bytes 1769480 | tf_op jit(solution)/shard_map/ppermute | solution.py:18
  19.8 5.1 %collective-permute-done.21.refs_3_ = f32[80,128]{1,0:T(8,128)S(1)} collective-permute-done((f32[80,128]{1,0:T(8,128)S(1)}, f32[80,128]{1,0:T(8,128)S(1)}, u32[]{:S(2)}, u32[]{:S(2)}) %collective-permute-start.21) | collective-permute-done | bytes 40992 | tf_op jit(solution)/shard_map/ppermute | solution.py:18
  28.7 2.6 %collective-permute-done.16 = f32[256,128]{1,0:T(8,128)S(1)} collective-permute-done((f32[256,128]{1,0:T(8,128)S(1)}, f32[256,128]{1,0:T(8,128)S(1)}, u32[]{:S(2)}, u32[]{:S(2)}) %collective-permute-start.16) | collective-permute-done | bytes 131104 | tf_op jit(solution)/shard_map/ppermute | solution.py:18
  31.2 2.6 %collective-permute-done.10.refs_9_ = f32[256,128]{1,0:T(8,128)S(1)} collective-permute-done((f32[256,128]{1,0:T(8,128)S(1)}, f32[256,128]{1,0:T(8,128)S(1)}, u32[]{:S(2)}, u32[]{:S(2)}) %collective-permute-start.10) | collective-permute-done | bytes 131104 | tf_op jit(solution)/shard_map/ppermute | solution.py:18
  35.2 2.1 %collective-permute-start.13 = (f32[256,128]{1,0:T(8,128)S(1)}, f32[256,128]{1,0:T(8,128)S(1)}, u32[]{:S(2)}, u32[]{:S(2)}) collective-permute-start(f32[256,128]{1,0:T(8,128)S(1)} %collective-permute-done.12), channel_id=1, source_target_pairs={{0,1},{1,0},{2,3},{3,2},{4,5},{5,4},{6,7},{7,6},{8,9},{9,8},{10,11... | collective-permute-start | bytes 393224 | tf_op jit(solution)/shard_map/ppermute | solution.py:18
  37.3 3.6 %collective-permute-done.8.refs_7_ = f32[256,128]{1,0:T(8,128)S(1)} collective-permute-done((f32[256,128]{1,0:T(8,128)S(1)}, f32[256,128]{1,0:T(8,128)S(1)}, u32[]{:S(2)}, u32[]{:S(2)}) %collective-permute-start.8) | collective-permute-done | bytes 131104 | tf_op jit(solution)/shard_map/ppermute | solution.py:18
  42.4 2.9 %collective-permute-start.7 = (f32[352,128]{1,0:T(8,128)S(1)}, f32[352,128]{1,0:T(8,128)S(1)}, u32[]{:S(2)}, u32[]{:S(2)}) collective-permute-start(f32[352,128]{1,0:T(8,128)S(1)} %get-tuple-element.49), channel_id=1, source_target_pairs={{0,3},{1,2},{2,1},{3,0},{4,7},{5,6},{6,5},{7,4},{8,11},{9,10},{10,... | collective-permute-start | bytes 540680 | tf_op jit(solution)/shard_map/ppermute | solution.py:18
  46.4 1.9 %collective-permute-start.17 = (f32[256,128]{1,0:T(8,128)S(1)}, f32[256,128]{1,0:T(8,128)S(1)}, u32[]{:S(2)}, u32[]{:S(2)}) collective-permute-start(f32[256,128]{1,0:T(8,128)S(1)} %collective-permute-done.16), channel_id=1, source_target_pairs={{0,3},{1,2},{2,1},{3,0},{4,7},{5,6},{6,5},{7,4},{8,11},{9,10},{10,... | collective-permute-start | bytes 393224 | tf_op jit(solution)/shard_map/ppermute | solution.py:18
  49.4 18.9 %collective-permute-done.15.refs_12_ = f32[256,128]{1,0:T(8,128)S(1)} collective-permute-done((f32[256,128]{1,0:T(8,128)S(1)}, f32[256,128]{1,0:T(8,128)S(1)}, u32[]{:S(2)}, u32[]{:S(2)}) %collective-permute-start.15) | collective-permute-done | bytes 131104 | tf_op jit(solution)/shard_map/ppermute | solution.py:18
  68.3 1.6 %shard_map.109 = (f32[864,128]{1,0:T(8,128)S(1)}, f32[288,128]{1,0:T(8,128)S(1)}) custom-call(f32[352,128]{1,0:T(8,128)S(1)} %get-tuple-element.46.refs_0_, f32[352,128]{1,0:T(8,128)S(1)} %collective-permute-done.5.refs_1_, f32[352,128]{1,0:T(8,128)S(1)} %collective-permute-done.6.refs_2_, f32[352,128]{1,0:T(8,128)S(1)} %collective-permute-done.7.refs_3_, ...), custom_call_target="tpu_custom_call" | custom-call | flops 603979776 | bytes 4685824 | tf_op jit(solution)/shard_map/pallas_call | solution.py:36
  71.2 7.0 %collective-permute-done.31.own = f32[288,128]{1,0:T(8,128)S(1)} collective-permute-done((f32[288,128]{1,0:T(8,128)S(1)}, f32[288,128]{1,0:T(8,128)S(1)}, u32[]{:S(2)}, u32[]{:S(2)}) %collective-permute-start.31) | collective-permute-done | bytes 147488 | tf_op jit(solution)/shard_map/ppermute | solution.py:18
  78.5 2.7 %collective-permute-start.29 = (f32[256,128]{1,0:T(8,128)S(1)}, f32[256,128]{1,0:T(8,128)S(1)}, u32[]{:S(2)}, u32[]{:S(2)}) collective-permute-start(f32[256,128]{1,0:T(8,128)S(1)} %get-tuple-element.73), channel_id=1, source_target_pairs={{0,8},{4,12},{8,0},{12,4},{1,9},{5,13},{9,1},{13,5},{2,10},{6,14},... | collective-permute-start | bytes 393224 | tf_op jit(solution)/shard_map/ppermute | solution.py:18
  81.5 2.0 %collective-permute-start.33 = (f32[256,128]{1,0:T(8,128)S(1)}, f32[256,128]{1,0:T(8,128)S(1)}, u32[]{:S(2)}, u32[]{:S(2)}) collective-permute-start(f32[256,128]{1,0:T(8,128)S(1)} %get-tuple-element.76), channel_id=1, source_target_pairs={{0,8},{4,12},{8,0},{12,4},{1,9},{5,13},{9,1},{13,5},{2,10},{6,14},... | collective-permute-start | bytes 393224 | tf_op jit(solution)/shard_map/ppermute | solution.py:18
  83.6 1.9 %collective-permute-done.29 = f32[256,128]{1,0:T(8,128)S(1)} collective-permute-done((f32[256,128]{1,0:T(8,128)S(1)}, f32[256,128]{1,0:T(8,128)S(1)}, u32[]{:S(2)}, u32[]{:S(2)}) %collective-permute-start.29) | collective-permute-done | bytes 131104 | tf_op jit(solution)/shard_map/ppermute | solution.py:18
  85.6 3.5 %collective-permute-start.30 = (f32[256,128]{1,0:T(8,128)S(1)}, f32[256,128]{1,0:T(8,128)S(1)}, u32[]{:S(2)}, u32[]{:S(2)}) collective-permute-start(f32[256,128]{1,0:T(8,128)S(1)} %add.25), channel_id=1, source_target_pairs={{0,2},{1,3},{2,0},{3,1},{4,6},{5,7},{6,4},{7,5},{8,10},{9,11},{10,... | collective-permute-start | bytes 393224 | tf_op jit(solution)/shard_map/ppermute | solution.py:18
  89.1 2.6 %collective-permute-start.28 = (f32[256,128]{1,0:T(8,128)S(1)}, f32[256,128]{1,0:T(8,128)S(1)}, u32[]{:S(2)}, u32[]{:S(2)}) collective-permute-start(f32[256,128]{1,0:T(8,128)S(1)} %add.24), channel_id=1, source_target_pairs={{0,1},{1,0},{2,3},{3,2},{4,5},{5,4},{6,7},{7,6},{8,9},{9,8},{10,11... | collective-permute-start | bytes 393224 | tf_op jit(solution)/shard_map/ppermute | solution.py:18
  95.9 1.5 %collective-permute-start.35 = (f32[256,128]{1,0:T(8,128)S(1)}, f32[256,128]{1,0:T(8,128)S(1)}, u32[]{:S(2)}, u32[]{:S(2)}) collective-permute-start(f32[256,128]{1,0:T(8,128)S(1)} %collective-permute-done.28.refs_1_), channel_id=1, source_target_pairs={{0,16},{16,0},{1,17},{17,1},{2,18},{18,2},{3,19},{19,3},{4,20},{20... | collective-permute-start | bytes 393224 | tf_op jit(solution)/shard_map/ppermute | solution.py:18
  97.4 2.9 %collective-permute-done.34.refs_4_ = f32[256,128]{1,0:T(8,128)S(1)} collective-permute-done((f32[256,128]{1,0:T(8,128)S(1)}, f32[256,128]{1,0:T(8,128)S(1)}, u32[]{:S(2)}, u32[]{:S(2)}) %collective-permute-start.34) | collective-permute-done | bytes 131104 | tf_op jit(solution)/shard_map/ppermute | solution.py:18
  100.3 2.8 %collective-permute-done.36.refs_6_ = f32[256,128]{1,0:T(8,128)S(1)} collective-permute-done((f32[256,128]{1,0:T(8,128)S(1)}, f32[256,128]{1,0:T(8,128)S(1)}, u32[]{:S(2)}, u32[]{:S(2)}) %collective-permute-start.36) | collective-permute-done | bytes 131104 | tf_op jit(solution)/shard_map/ppermute | solution.py:18
  103.1 2.1 %collective-permute-done.35.refs_5_ = f32[256,128]{1,0:T(8,128)S(1)} collective-permute-done((f32[256,128]{1,0:T(8,128)S(1)}, f32[256,128]{1,0:T(8,128)S(1)}, u32[]{:S(2)}, u32[]{:S(2)}) %collective-permute-start.35) | collective-permute-done | bytes 131104 | tf_op jit(solution)/shard_map/ppermute | solution.py:18
  (94 shorter events, 23.7 us)
Async XLA Ops:
  1.1 9.3 %collective-permute-start.3 = (f32[1024,128]{1,0:T(8,128)S(1)}, f32[1024,128]{1,0:T(8,128)S(1)}, u32[]{:S(2)}, u32[]{:S(2)}) collective-permute-start(f32[1024,128]{1,0:T(8,128)S(1)} %bitcast.22), channel_id=1, source_target_pairs={{0,4},{4,0},{8,12},{12,8},{1,5},{5,1},{9,13},{13,9},{2,6},{6,2},{1... | collective-permute-start | bytes 1572872 | tf_op jit(solution)/shard_map/ppermute | solution.py:18
  2.3 10.0 %collective-permute-start = (f32[128,128]{1,0:T(8,128)S(1)}, f32[128,128]{1,0:T(8,128)S(1)}, u32[]{:S(2)}, u32[]{:S(2)}) collective-permute-start(f32[128,128]{1,0:T(8,128)S(1)} %get-tuple-element.82), channel_id=1, source_target_pairs={{0,4},{4,0},{8,12},{12,8},{1,5},{5,1},{9,13},{13,9},{2,6},{6,2},{1... | collective-permute-start | bytes 196616 | tf_op jit(solution)/shard_map/ppermute | solution.py:18
  2.9 12.1 %collective-permute-start.1 = (f32[128,128]{1,0:T(8,128)S(1)}, f32[128,128]{1,0:T(8,128)S(1)}, u32[]{:S(2)}, u32[]{:S(2)}) collective-permute-start(f32[128,128]{1,0:T(8,128)S(1)} %get-tuple-element.81), channel_id=1, source_target_pairs={{4,8},{8,4},{5,9},{9,5},{6,10},{10,6},{7,11},{11,7},{20,24},{24,20... | collective-permute-start | bytes 196616 | tf_op jit(solution)/shard_map/ppermute | solution.py:501
  6.7 20.3 %collective-permute-start.12 = (f32[256,128]{1,0:T(8,128)S(1)}, f32[256,128]{1,0:T(8,128)S(1)}, u32[]{:S(2)}, u32[]{:S(2)}) collective-permute-start(f32[256,128]{1,0:T(8,128)S(1)} %get-tuple-element.57), channel_id=1, source_target_pairs={{0,16},{16,0},{1,17},{17,1},{2,18},{18,2},{3,19},{19,3},{4,20},{20... | collective-permute-start | bytes 393224 | tf_op jit(solution)/shard_map/ppermute | solution.py:18
  8.3 19.4 %collective-permute-start.14 = (f32[256,128]{1,0:T(8,128)S(1)}, f32[256,128]{1,0:T(8,128)S(1)}, u32[]{:S(2)}, u32[]{:S(2)}) collective-permute-start(f32[256,128]{1,0:T(8,128)S(1)} %get-tuple-element.58), channel_id=1, source_target_pairs={{0,16},{16,0},{1,17},{17,1},{2,18},{18,2},{3,19},{19,3},{4,20},{20... | collective-permute-start | bytes 393224 | tf_op jit(solution)/shard_map/ppermute | solution.py:18
  10.4 8.0 %collective-permute-start.19 = (f32[80,128]{1,0:T(8,128)S(1)}, f32[80,128]{1,0:T(8,128)S(1)}, u32[]{:S(2)}, u32[]{:S(2)}) collective-permute-start(f32[80,128]{1,0:T(8,128)S(1)} %shard_map.106.refs_0_), channel_id=1, source_target_pairs={{0,1},{1,0},{2,3},{3,2},{4,5},{5,4},{6,7},{7,6},{8,9},{9,8},{10,11... | collective-permute-start | bytes 122888 | tf_op jit(solution)/shard_map/ppermute | solution.py:18
  15.0 20.2 %collective-permute-start.4 = (f32[1152,128]{1,0:T(8,128)S(1)}, f32[1152,128]{1,0:T(8,128)S(1)}, u32[]{:S(2)}, u32[]{:S(2)}) collective-permute-start(f32[1152,128]{1,0:T(8,128)S(1)} %get-tuple-element.45), channel_id=1, source_target_pairs={{0,8},{4,12},{8,0},{12,4},{1,9},{5,13},{9,1},{13,5},{2,10},{6,14},... | collective-permute-start | bytes 1769480 | tf_op jit(solution)/shard_map/ppermute | solution.py:18
  18.4 7.9 %collective-permute-start.2 = (f32[4,32,128]{2,1,0:T(8,128)S(1)}, f32[4,32,128]{2,1,0:T(8,128)S(1)}, u32[]{:S(2)}, u32[]{:S(2)}) collective-permute-start(f32[4,32,128]{2,1,0:T(8,128)S(1)} %bitcast.34), channel_id=1, source_target_pairs={{0,16},{16,0},{1,17},{17,1},{2,18},{18,2},{3,19},{19,3},{4,20},{20... | collective-permute-start | bytes 196616 | tf_op jit(solution)/shard_map/ppermute | solution.py:18
  26.3 8.8 %collective-permute-start.23 = (f32[4,80,128]{2,1,0:T(8,128)S(1)}, f32[4,80,128]{2,1,0:T(8,128)S(1)}, u32[]{:S(2)}, u32[]{:S(2)}) collective-permute-start(f32[4,80,128]{2,1,0:T(8,128)S(1)} %shard_map.107.refs_0_.refs_4_), channel_id=1, source_target_pairs={{0,16},{16,0},{1,17},{17,1},{2,18},{18,2},{3,19},{19,3},{4,20},{20... | collective-permute-start | bytes 491528 | tf_op jit(solution)/shard_map/ppermute | solution.py:18
  31.2 11.1 %collective-permute-start.22 = (f32[4,80,128]{2,1,0:T(8,128)S(1)}, f32[4,80,128]{2,1,0:T(8,128)S(1)}, u32[]{:S(2)}, u32[]{:S(2)}) collective-permute-start(f32[4,80,128]{2,1,0:T(8,128)S(1)} %shard_map.107.refs_0_.refs_4_), channel_id=1, source_target_pairs={{0,4},{4,0},{8,12},{12,8},{1,5},{5,1},{9,13},{13,9},{2,6},{6,2},{1... | collective-permute-start | bytes 491528 | tf_op jit(solution)/shard_map/ppermute | solution.py:18
  35.2 11.3 %collective-permute-start.24 = (f32[4,80,128]{2,1,0:T(8,128)S(1)}, f32[4,80,128]{2,1,0:T(8,128)S(1)}, u32[]{:S(2)}, u32[]{:S(2)}) collective-permute-start(f32[4,80,128]{2,1,0:T(8,128)S(1)} %collective-permute-done.23.refs_2_.refs_5_), channel_id=1, source_target_pairs={{0,4},{4,0},{8,12},{12,8},{1,5},{5,1},{9,13},{13,9},{2,6},{6,2},{1... | collective-permute-start | bytes 491528 | tf_op jit(solution)/shard_map/ppermute | solution.py:18
  35.2 11.3 %collective-permute-start.13 = (f32[256,128]{1,0:T(8,128)S(1)}, f32[256,128]{1,0:T(8,128)S(1)}, u32[]{:S(2)}, u32[]{:S(2)}) collective-permute-start(f32[256,128]{1,0:T(8,128)S(1)} %collective-permute-done.12), channel_id=1, source_target_pairs={{0,1},{1,0},{2,3},{3,2},{4,5},{5,4},{6,7},{7,6},{8,9},{9,8},{10,11... | collective-permute-start | bytes 393224 | tf_op jit(solution)/shard_map/ppermute | solution.py:18
  40.9 27.3 %collective-permute-start.5 = (f32[352,128]{1,0:T(8,128)S(1)}, f32[352,128]{1,0:T(8,128)S(1)}, u32[]{:S(2)}, u32[]{:S(2)}) collective-permute-start(f32[352,128]{1,0:T(8,128)S(1)} %get-tuple-element.47), channel_id=1, source_target_pairs={{0,1},{1,0},{2,3},{3,2},{4,5},{5,4},{6,7},{7,6},{8,9},{9,8},{10,11... | collective-permute-start | bytes 540680 | tf_op jit(solution)/shard_map/ppermute | solution.py:18
  42.4 25.9 %collective-permute-start.6 = (f32[352,128]{1,0:T(8,128)S(1)}, f32[352,128]{1,0:T(8,128)S(1)}, u32[]{:S(2)}, u32[]{:S(2)}) collective-permute-start(f32[352,128]{1,0:T(8,128)S(1)} %get-tuple-element.48), channel_id=1, source_target_pairs={{0,2},{1,3},{2,0},{3,1},{4,6},{5,7},{6,4},{7,5},{8,10},{9,11},{10,... | collective-permute-start | bytes 540680 | tf_op jit(solution)/shard_map/ppermute | solution.py:18
  42.4 25.9 %collective-permute-start.7 = (f32[352,128]{1,0:T(8,128)S(1)}, f32[352,128]{1,0:T(8,128)S(1)}, u32[]{:S(2)}, u32[]{:S(2)}) collective-permute-start(f32[352,128]{1,0:T(8,128)S(1)} %get-tuple-element.49), channel_id=1, source_target_pairs={{0,3},{1,2},{2,1},{3,0},{4,7},{5,6},{6,5},{7,4},{8,11},{9,10},{10,... | collective-permute-start | bytes 540680 | tf_op jit(solution)/shard_map/ppermute | solution.py:18
  46.4 21.8 %collective-permute-start.15 = (f32[256,128]{1,0:T(8,128)S(1)}, f32[256,128]{1,0:T(8,128)S(1)}, u32[]{:S(2)}, u32[]{:S(2)}) collective-permute-start(f32[256,128]{1,0:T(8,128)S(1)} %collective-permute-done.14), channel_id=1, source_target_pairs={{0,2},{1,3},{2,0},{3,1},{4,6},{5,7},{6,4},{7,5},{8,10},{9,11},{10,... | collective-permute-start | bytes 393224 | tf_op jit(solution)/shard_map/ppermute | solution.py:18
  46.4 21.8 %collective-permute-start.17 = (f32[256,128]{1,0:T(8,128)S(1)}, f32[256,128]{1,0:T(8,128)S(1)}, u32[]{:S(2)}, u32[]{:S(2)}) collective-permute-start(f32[256,128]{1,0:T(8,128)S(1)} %collective-permute-done.16), channel_id=1, source_target_pairs={{0,3},{1,2},{2,1},{3,0},{4,7},{5,6},{6,5},{7,4},{8,11},{9,10},{10,... | collective-permute-start | bytes 393224 | tf_op jit(solution)/shard_map/ppermute | solution.py:18
  69.9 8.2 %collective-permute-start.25 = (f32[864,128]{1,0:T(8,128)S(1)}, f32[864,128]{1,0:T(8,128)S(1)}, u32[]{:S(2)}, u32[]{:S(2)}) collective-permute-start(f32[864,128]{1,0:T(8,128)S(1)} %get-tuple-element.66.own), channel_id=1, source_target_pairs={{0,4},{4,0},{8,12},{12,8},{1,5},{5,1},{9,13},{13,9},{2,6},{6,2},{1... | collective-permute-start | bytes 1327112 | tf_op jit(solution)/shard_map/ppermute | solution.py:18
  70.0 8.2 %collective-permute-start.31 = (f32[288,128]{1,0:T(8,128)S(1)}, f32[288,128]{1,0:T(8,128)S(1)}, u32[]{:S(2)}, u32[]{:S(2)}) collective-permute-start(f32[288,128]{1,0:T(8,128)S(1)} %get-tuple-element.74), channel_id=1, source_target_pairs={{0,3},{1,2},{2,1},{3,0},{4,7},{5,6},{6,5},{7,4},{8,11},{9,10},{10,... | collective-permute-start | bytes 442376 | tf_op jit(solution)/shard_map/ppermute | solution.py:18
  81.2 7.8 %collective-permute-start.27 = (f32[256,128]{1,0:T(8,128)S(1)}, f32[256,128]{1,0:T(8,128)S(1)}, u32[]{:S(2)}, u32[]{:S(2)}) collective-permute-start(f32[256,128]{1,0:T(8,128)S(1)} %get-tuple-element.71), channel_id=1, source_target_pairs={{0,8},{4,12},{8,0},{12,4},{1,9},{5,13},{9,1},{13,5},{2,10},{6,14},... | collective-permute-start | bytes 393224 | tf_op jit(solution)/shard_map/ppermute | solution.py:18
  81.5 10.1 %collective-permute-start.33 = (f32[256,128]{1,0:T(8,128)S(1)}, f32[256,128]{1,0:T(8,128)S(1)}, u32[]{:S(2)}, u32[]{:S(2)}) collective-permute-start(f32[256,128]{1,0:T(8,128)S(1)} %get-tuple-element.76), channel_id=1, source_target_pairs={{0,8},{4,12},{8,0},{12,4},{1,9},{5,13},{9,1},{13,5},{2,10},{6,14},... | collective-permute-start | bytes 393224 | tf_op jit(solution)/shard_map/ppermute | solution.py:18
  83.5 10.3 %collective-permute-start.26 = (f32[256,128]{1,0:T(8,128)S(1)}, f32[256,128]{1,0:T(8,128)S(1)}, u32[]{:S(2)}, u32[]{:S(2)}) collective-permute-start(f32[256,128]{1,0:T(8,128)S(1)} %get-tuple-element.69), channel_id=1, source_target_pairs={{0,8},{4,12},{8,0},{12,4},{1,9},{5,13},{9,1},{13,5},{2,10},{6,14},... | collective-permute-start | bytes 393224 | tf_op jit(solution)/shard_map/ppermute | solution.py:18
  85.6 9.8 %collective-permute-start.30 = (f32[256,128]{1,0:T(8,128)S(1)}, f32[256,128]{1,0:T(8,128)S(1)}, u32[]{:S(2)}, u32[]{:S(2)}) collective-permute-start(f32[256,128]{1,0:T(8,128)S(1)} %add.25), channel_id=1, source_target_pairs={{0,2},{1,3},{2,0},{3,1},{4,6},{5,7},{6,4},{7,5},{8,10},{9,11},{10,... | collective-permute-start | bytes 393224 | tf_op jit(solution)/shard_map/ppermute | solution.py:18
  95.9 9.2 %collective-permute-start.35 = (f32[256,128]{1,0:T(8,128)S(1)}, f32[256,128]{1,0:T(8,128)S(1)}, u32[]{:S(2)}, u32[]{:S(2)}) collective-permute-start(f32[256,128]{1,0:T(8,128)S(1)} %collective-permute-done.28.refs_1_), channel_id=1, source_target_pairs={{0,16},{16,0},{1,17},{17,1},{2,18},{18,2},{3,19},{19,3},{4,20},{20... | collective-permute-start | bytes 393224 | tf_op jit(solution)/shard_map/ppermute | solution.py:18
  (24 other events, 151.2 us)

commit v2 on v1

--- a/solution.py
+++ b/solution.py
@@ -338,7 +338,7 @@
     result = dot(high, part) + dot(low, part)
     tall = fields + 2 * group * share
     for k in range(bands):
-        out, at = (outs[1], 0) if len(outs) > 1 and k == bands - 1 else (outs[0], k * tall)
+        out, at = (outs[1 + k // 2], 0) if k % 2 else (outs[0], k // 2 * tall)
         out[at : at + tall, :] = result[:, k * width : (k + 1) * width]
 
 
@@ -565,7 +565,7 @@
     )
     flops = 4 * tall * whole * whole
     scratch = [pltpu.VMEM((lons, window_rows, width), F32)] * 2
-    early = max(lons - 1, 1)
+    early = (lons + 1) // 2
     shapes = [struct(early * tall, width)] + [struct(tall, width)] * (lons - early)
     if parts == 1:
         spread = vmem_call(
@@ -615,11 +615,11 @@
         return pieces
 
     done = {}
-    for k, piece in enumerate(lat_back(spread[0], early)):
-        done[k] = swap(piece, "lon", k) if k > 0 else piece
-    if early < lons:
-        piece = swap(spread[1], "lon", early)
-        [done[early]] = lat_back(piece, 1)
+    for n, piece in enumerate(lat_back(spread[0], early)):
+        done[2 * n] = swap(piece, "lon", 2 * n) if n > 0 else piece
+    for k in range(1, lons, 2):
+        piece = swap(spread[1 + k // 2], "lon", k)
+        [done[k]] = lat_back(piece, 1)
     arrived = {}
     for k in done:
         arrived[k, 0] = done[k]

time: 107 us -> 106 us (level)
  starting transfers between devices: 43.3 us -> 39.8 us
  waiting for transfers between devices: 54.7 us -> 57.5 us
    ppermute x37 -> x38, starting transfers between devices: 42.6 us -> 39.1 us  [swap(): lax.ppermute(x, axis, [(i, i ^ k) for i in range(lax.axis_size(axis))])]
    ppermute x37 -> x38, waiting for transfers between devices: 54.7 us -> 57.5 us  [swap(): lax.ppermute(x, axis, [(i, i ^ k) for i in range(lax.axis_size(axis))])]
    pallas_call x13 -> x14, Pallas kernels: 6.27 us -> 6.44 us  [vmem_call(): pl.pallas_call(kernel, out_shape=out_shape, in_specs=specs, out_specs=[pl...]
  transfers between devices with their start and end apart: 38 -> 39, of which waited for: 16 -> 18; matrix products, arithmetic and copies ran while one was open for 0% -> 0% of each run, Pallas kernels for 3% -> 4%
where the time goes in v2:
time: 106 us
  waiting for transfers between devices  57.5 us (54%)
  starting transfers between devices  39.8 us (38%)
  Pallas kernels  6.44 us (6%)
  local copies, waits for them, and re-layouts  1.61 us (2%)
    ppermute x38, waiting for transfers between devices, swap(): lax.ppermute(x, axis, [(i, i ^ k) for i in range(lax.axis_size(axis))])  57.5 us
    ppermute x38, starting transfers between devices, swap(): lax.ppermute(x, axis, [(i, i ^ k) for i in range(lax.axis_size(axis))])  39.1 us
    pallas_call x14, Pallas kernels, vmem_call(): pl.pallas_call(kernel, out_shape=out_shape, in_specs=specs, out_specs=[pl...  6.44 us
  transfers between devices with their start and end apart: 39, of which 18 were waited for; matrix products, arithmetic and copies ran while one was open for 0% of the time, Pallas kernels for 4%

profile of v2, /device:TPU:0, one launch (start us, length us, event | category | flops | bytes accessed | tf_op | source)
XLA Modules:
  0.0 105.7 jit_solution(18315051640092186644)
XLA Ops:
  4.2 2.6 %collective-permute-start.18 = (f32[8,64]{1,0:T(8,128)S(1)}, f32[8,64]{1,0:T(8,128)S(1)}, u32[]{:S(2)}, u32[]{:S(2)}) collective-permute-start(f32[8,64]{1,0:T(8,128)S(1)} %get-tuple-element.62), channel_id=1, source_target_pairs={{0,16},{16,0},{1,17},{17,1},{2,18},{18,2},{3,19},{19,3},{4,20},{20... | collective-permute-start | bytes 6152 | tf_op jit(solution)/shard_map/ppermute | solution.py:18
  8.3 2.0 %collective-permute-start.14 = (f32[256,128]{1,0:T(8,128)S(1)}, f32[256,128]{1,0:T(8,128)S(1)}, u32[]{:S(2)}, u32[]{:S(2)}) collective-permute-start(f32[256,128]{1,0:T(8,128)S(1)} %get-tuple-element.59), channel_id=1, source_target_pairs={{0,16},{16,0},{1,17},{17,1},{2,18},{18,2},{3,19},{19,3},{4,20},{20... | collective-permute-start | bytes 393224 | tf_op jit(solution)/shard_map/ppermute | solution.py:18
  10.4 1.6 %collective-permute-start.19 = (f32[80,128]{1,0:T(8,128)S(1)}, f32[80,128]{1,0:T(8,128)S(1)}, u32[]{:S(2)}, u32[]{:S(2)}) collective-permute-start(f32[80,128]{1,0:T(8,128)S(1)} %shard_map.106.refs_0_), channel_id=1, source_target_pairs={{0,1},{1,0},{2,3},{3,2},{4,5},{5,4},{6,7},{7,6},{8,9},{9,8},{10,11... | collective-permute-start | bytes 122888 | tf_op jit(solution)/shard_map/ppermute | solution.py:18
  12.4 2.6 %collective-permute-start.20 = (f32[80,128]{1,0:T(8,128)S(1)}, f32[80,128]{1,0:T(8,128)S(1)}, u32[]{:S(2)}, u32[]{:S(2)}) collective-permute-start(f32[80,128]{1,0:T(8,128)S(1)} %shard_map.106.refs_0_), channel_id=1, source_target_pairs={{0,2},{1,3},{2,0},{3,1},{4,6},{5,7},{6,4},{7,5},{8,10},{9,11},{10,... | collective-permute-start | bytes 122888 | tf_op jit(solution)/shard_map/ppermute | solution.py:18
  15.0 3.4 %collective-permute-start.4 = (f32[1152,128]{1,0:T(8,128)S(1)}, f32[1152,128]{1,0:T(8,128)S(1)}, u32[]{:S(2)}, u32[]{:S(2)}) collective-permute-start(f32[1152,128]{1,0:T(8,128)S(1)} %get-tuple-element.46), channel_id=1, source_target_pairs={{0,8},{4,12},{8,0},{12,4},{1,9},{5,13},{9,1},{13,5},{2,10},{6,14},... | collective-permute-start | bytes 1769480 | tf_op jit(solution)/shard_map/ppermute | solution.py:18
  19.8 5.1 %collective-permute-done.21.refs_3_ = f32[80,128]{1,0:T(8,128)S(1)} collective-permute-done((f32[80,128]{1,0:T(8,128)S(1)}, f32[80,128]{1,0:T(8,128)S(1)}, u32[]{:S(2)}, u32[]{:S(2)}) %collective-permute-start.21) | collective-permute-done | bytes 40992 | tf_op jit(solution)/shard_map/ppermute | solution.py:18
  24.9 1.5 %collective-permute-start.16 = (f32[256,128]{1,0:T(8,128)S(1)}, f32[256,128]{1,0:T(8,128)S(1)}, u32[]{:S(2)}, u32[]{:S(2)}) collective-permute-start(f32[256,128]{1,0:T(8,128)S(1)} %get-tuple-element.60), channel_id=1, source_target_pairs={{0,16},{16,0},{1,17},{17,1},{2,18},{18,2},{3,19},{19,3},{4,20},{20... | collective-permute-start | bytes 393224 | tf_op jit(solution)/shard_map/ppermute | solution.py:18
  28.7 2.6 %collective-permute-done.16 = f32[256,128]{1,0:T(8,128)S(1)} collective-permute-done((f32[256,128]{1,0:T(8,128)S(1)}, f32[256,128]{1,0:T(8,128)S(1)}, u32[]{:S(2)}, u32[]{:S(2)}) %collective-permute-start.16) | collective-permute-done | bytes 131104 | tf_op jit(solution)/shard_map/ppermute | solution.py:18
  31.2 2.6 %collective-permute-done.10.refs_9_ = f32[256,128]{1,0:T(8,128)S(1)} collective-permute-done((f32[256,128]{1,0:T(8,128)S(1)}, f32[256,128]{1,0:T(8,128)S(1)}, u32[]{:S(2)}, u32[]{:S(2)}) %collective-permute-start.10) | collective-permute-done | bytes 131104 | tf_op jit(solution)/shard_map/ppermute | solution.py:18
  35.2 2.1 %collective-permute-start.13 = (f32[256,128]{1,0:T(8,128)S(1)}, f32[256,128]{1,0:T(8,128)S(1)}, u32[]{:S(2)}, u32[]{:S(2)}) collective-permute-start(f32[256,128]{1,0:T(8,128)S(1)} %collective-permute-done.12), channel_id=1, source_target_pairs={{0,1},{1,0},{2,3},{3,2},{4,5},{5,4},{6,7},{7,6},{8,9},{9,8},{10,11... | collective-permute-start | bytes 393224 | tf_op jit(solution)/shard_map/ppermute | solution.py:18
  37.3 3.6 %collective-permute-done.8.refs_7_ = f32[256,128]{1,0:T(8,128)S(1)} collective-permute-done((f32[256,128]{1,0:T(8,128)S(1)}, f32[256,128]{1,0:T(8,128)S(1)}, u32[]{:S(2)}, u32[]{:S(2)}) %collective-permute-start.8) | collective-permute-done | bytes 131104 | tf_op jit(solution)/shard_map/ppermute | solution.py:18
  42.4 2.9 %collective-permute-start.7 = (f32[352,128]{1,0:T(8,128)S(1)}, f32[352,128]{1,0:T(8,128)S(1)}, u32[]{:S(2)}, u32[]{:S(2)}) collective-permute-start(f32[352,128]{1,0:T(8,128)S(1)} %get-tuple-element.50), channel_id=1, source_target_pairs={{0,3},{1,2},{2,1},{3,0},{4,7},{5,6},{6,5},{7,4},{8,11},{9,10},{10,... | collective-permute-start | bytes 540680 | tf_op jit(solution)/shard_map/ppermute | solution.py:18
  46.4 1.9 %collective-permute-start.17 = (f32[256,128]{1,0:T(8,128)S(1)}, f32[256,128]{1,0:T(8,128)S(1)}, u32[]{:S(2)}, u32[]{:S(2)}) collective-permute-start(f32[256,128]{1,0:T(8,128)S(1)} %collective-permute-done.16), channel_id=1, source_target_pairs={{0,3},{1,2},{2,1},{3,0},{4,7},{5,6},{6,5},{7,4},{8,11},{9,10},{10,... | collective-permute-start | bytes 393224 | tf_op jit(solution)/shard_map/ppermute | solution.py:18
  49.4 18.9 %collective-permute-done.15.refs_12_ = f32[256,128]{1,0:T(8,128)S(1)} collective-permute-done((f32[256,128]{1,0:T(8,128)S(1)}, f32[256,128]{1,0:T(8,128)S(1)}, u32[]{:S(2)}, u32[]{:S(2)}) %collective-permute-start.15) | collective-permute-done | bytes 131104 | tf_op jit(solution)/shard_map/ppermute | solution.py:18
  68.3 1.6 %shard_map.109 = (f32[576,128]{1,0:T(8,128)S(1)}, f32[288,128]{1,0:T(8,128)S(1)}, f32[288,128]{1,0:T(8,128)S(1)}) custom-call(f32[352,128]{1,0:T(8,128)S(1)} %get-tuple-element.47.refs_0_, f32[352,128]{1,0:T(8,128)S(1)} %collective-permute-done.5.refs_1_, f32[352,128]{1,0:T(8,128)S(1)} %collective-permute-done.6.refs_2_, ...), custom_call_target="tpu_custom_call" | custom-call | flops 603979776 | bytes 4685824 | tf_op jit(solution)/shard_map/pallas_call | solution.py:36
  72.3 6.4 %collective-permute-done.32.own = f32[288,128]{1,0:T(8,128)S(1)} collective-permute-done((f32[288,128]{1,0:T(8,128)S(1)}, f32[288,128]{1,0:T(8,128)S(1)}, u32[]{:S(2)}, u32[]{:S(2)}) %collective-permute-start.32) | collective-permute-done | bytes 147488 | tf_op jit(solution)/shard_map/ppermute | solution.py:18
  78.6 1.6 %collective-permute-done.27.own = f32[288,128]{1,0:T(8,128)S(1)} collective-permute-done((f32[288,128]{1,0:T(8,128)S(1)}, f32[288,128]{1,0:T(8,128)S(1)}, u32[]{:S(2)}, u32[]{:S(2)}) %collective-permute-start.27) | collective-permute-done | bytes 147488 | tf_op jit(solution)/shard_map/ppermute | solution.py:18
  80.6 3.2 %collective-permute-start.30 = (f32[256,128]{1,0:T(8,128)S(1)}, f32[256,128]{1,0:T(8,128)S(1)}, u32[]{:S(2)}, u32[]{:S(2)}) collective-permute-start(f32[256,128]{1,0:T(8,128)S(1)} %get-tuple-element.75), channel_id=1, source_target_pairs={{0,8},{4,12},{8,0},{12,4},{1,9},{5,13},{9,1},{13,5},{2,10},{6,14},... | collective-permute-start | bytes 393224 | tf_op jit(solution)/shard_map/ppermute | solution.py:18
  84.3 2.1 %collective-permute-start.29 = (f32[256,128]{1,0:T(8,128)S(1)}, f32[256,128]{1,0:T(8,128)S(1)}, u32[]{:S(2)}, u32[]{:S(2)}) collective-permute-start(f32[256,128]{1,0:T(8,128)S(1)} %get-tuple-element.73), channel_id=1, source_target_pairs={{0,8},{4,12},{8,0},{12,4},{1,9},{5,13},{9,1},{13,5},{2,10},{6,14},... | collective-permute-start | bytes 393224 | tf_op jit(solution)/shard_map/ppermute | solution.py:18
  86.5 1.6 %collective-permute-done.30 = f32[256,128]{1,0:T(8,128)S(1)} collective-permute-done((f32[256,128]{1,0:T(8,128)S(1)}, f32[256,128]{1,0:T(8,128)S(1)}, u32[]{:S(2)}, u32[]{:S(2)}) %collective-permute-start.30) | collective-permute-done | bytes 131104 | tf_op jit(solution)/shard_map/ppermute | solution.py:18
  92.0 1.7 %collective-permute-done.29 = f32[256,128]{1,0:T(8,128)S(1)} collective-permute-done((f32[256,128]{1,0:T(8,128)S(1)}, f32[256,128]{1,0:T(8,128)S(1)}, u32[]{:S(2)}, u32[]{:S(2)}) %collective-permute-start.29) | collective-permute-done | bytes 131104 | tf_op jit(solution)/shard_map/ppermute | solution.py:18
  94.8 1.5 %collective-permute-done.26 = f32[256,128]{1,0:T(8,128)S(1)} collective-permute-done((f32[256,128]{1,0:T(8,128)S(1)}, f32[256,128]{1,0:T(8,128)S(1)}, u32[]{:S(2)}, u32[]{:S(2)}) %collective-permute-start.26) | collective-permute-done | bytes 131104 | tf_op jit(solution)/shard_map/ppermute | solution.py:18
  99.0 3.8 %collective-permute-done.35.refs_4_ = f32[256,128]{1,0:T(8,128)S(1)} collective-permute-done((f32[256,128]{1,0:T(8,128)S(1)}, f32[256,128]{1,0:T(8,128)S(1)}, u32[]{:S(2)}, u32[]{:S(2)}) %collective-permute-start.35) | collective-permute-done | bytes 131104 | tf_op jit(solution)/shard_map/ppermute | solution.py:18
  102.8 1.8 %collective-permute-done.37.refs_6_ = f32[256,128]{1,0:T(8,128)S(1)} collective-permute-done((f32[256,128]{1,0:T(8,128)S(1)}, f32[256,128]{1,0:T(8,128)S(1)}, u32[]{:S(2)}, u32[]{:S(2)}) %collective-permute-start.37) | collective-permute-done | bytes 131104 | tf_op jit(solution)/shard_map/ppermute | solution.py:18
  (97 shorter events, 26.8 us)
Async XLA Ops:
  1.1 9.3 %collective-permute-start.3 = (f32[1024,128]{1,0:T(8,128)S(1)}, f32[1024,128]{1,0:T(8,128)S(1)}, u32[]{:S(2)}, u32[]{:S(2)}) collective-permute-start(f32[1024,128]{1,0:T(8,128)S(1)} %bitcast.22), channel_id=1, source_target_pairs={{0,4},{4,0},{8,12},{12,8},{1,5},{5,1},{9,13},{13,9},{2,6},{6,2},{1... | collective-permute-start | bytes 1572872 | tf_op jit(solution)/shard_map/ppermute | solution.py:18
  2.3 10.0 %collective-permute-start = (f32[128,128]{1,0:T(8,128)S(1)}, f32[128,128]{1,0:T(8,128)S(1)}, u32[]{:S(2)}, u32[]{:S(2)}) collective-permute-start(f32[128,128]{1,0:T(8,128)S(1)} %get-tuple-element.84), channel_id=1, source_target_pairs={{0,4},{4,0},{8,12},{12,8},{1,5},{5,1},{9,13},{13,9},{2,6},{6,2},{1... | collective-permute-start | bytes 196616 | tf_op jit(solution)/shard_map/ppermute | solution.py:18
  2.9 12.1 %collective-permute-start.1 = (f32[128,128]{1,0:T(8,128)S(1)}, f32[128,128]{1,0:T(8,128)S(1)}, u32[]{:S(2)}, u32[]{:S(2)}) collective-permute-start(f32[128,128]{1,0:T(8,128)S(1)} %get-tuple-element.83), channel_id=1, source_target_pairs={{4,8},{8,4},{5,9},{9,5},{6,10},{10,6},{7,11},{11,7},{20,24},{24,20... | collective-permute-start | bytes 196616 | tf_op jit(solution)/shard_map/ppermute | solution.py:501
  6.7 20.3 %collective-permute-start.12 = (f32[256,128]{1,0:T(8,128)S(1)}, f32[256,128]{1,0:T(8,128)S(1)}, u32[]{:S(2)}, u32[]{:S(2)}) collective-permute-start(f32[256,128]{1,0:T(8,128)S(1)} %get-tuple-element.58), channel_id=1, source_target_pairs={{0,16},{16,0},{1,17},{17,1},{2,18},{18,2},{3,19},{19,3},{4,20},{20... | collective-permute-start | bytes 393224 | tf_op jit(solution)/shard_map/ppermute | solution.py:18
  8.3 19.4 %collective-permute-start.14 = (f32[256,128]{1,0:T(8,128)S(1)}, f32[256,128]{1,0:T(8,128)S(1)}, u32[]{:S(2)}, u32[]{:S(2)}) collective-permute-start(f32[256,128]{1,0:T(8,128)S(1)} %get-tuple-element.59), channel_id=1, source_target_pairs={{0,16},{16,0},{1,17},{17,1},{2,18},{18,2},{3,19},{19,3},{4,20},{20... | collective-permute-start | bytes 393224 | tf_op jit(solution)/shard_map/ppermute | solution.py:18
  10.4 8.0 %collective-permute-start.19 = (f32[80,128]{1,0:T(8,128)S(1)}, f32[80,128]{1,0:T(8,128)S(1)}, u32[]{:S(2)}, u32[]{:S(2)}) collective-permute-start(f32[80,128]{1,0:T(8,128)S(1)} %shard_map.106.refs_0_), channel_id=1, source_target_pairs={{0,1},{1,0},{2,3},{3,2},{4,5},{5,4},{6,7},{7,6},{8,9},{9,8},{10,11... | collective-permute-start | bytes 122888 | tf_op jit(solution)/shard_map/ppermute | solution.py:18
  15.0 20.2 %collective-permute-start.4 = (f32[1152,128]{1,0:T(8,128)S(1)}, f32[1152,128]{1,0:T(8,128)S(1)}, u32[]{:S(2)}, u32[]{:S(2)}) collective-permute-start(f32[1152,128]{1,0:T(8,128)S(1)} %get-tuple-element.46), channel_id=1, source_target_pairs={{0,8},{4,12},{8,0},{12,4},{1,9},{5,13},{9,1},{13,5},{2,10},{6,14},... | collective-permute-start | bytes 1769480 | tf_op jit(solution)/shard_map/ppermute | solution.py:18
  18.4 7.9 %collective-permute-start.2 = (f32[4,32,128]{2,1,0:T(8,128)S(1)}, f32[4,32,128]{2,1,0:T(8,128)S(1)}, u32[]{:S(2)}, u32[]{:S(2)}) collective-permute-start(f32[4,32,128]{2,1,0:T(8,128)S(1)} %bitcast.34), channel_id=1, source_target_pairs={{0,16},{16,0},{1,17},{17,1},{2,18},{18,2},{3,19},{19,3},{4,20},{20... | collective-permute-start | bytes 196616 | tf_op jit(solution)/shard_map/ppermute | solution.py:18
  26.3 8.8 %collective-permute-start.23 = (f32[4,80,128]{2,1,0:T(8,128)S(1)}, f32[4,80,128]{2,1,0:T(8,128)S(1)}, u32[]{:S(2)}, u32[]{:S(2)}) collective-permute-start(f32[4,80,128]{2,1,0:T(8,128)S(1)} %shard_map.107.refs_0_.refs_4_), channel_id=1, source_target_pairs={{0,16},{16,0},{1,17},{17,1},{2,18},{18,2},{3,19},{19,3},{4,20},{20... | collective-permute-start | bytes 491528 | tf_op jit(solution)/shard_map/ppermute | solution.py:18
  31.2 11.1 %collective-permute-start.22 = (f32[4,80,128]{2,1,0:T(8,128)S(1)}, f32[4,80,128]{2,1,0:T(8,128)S(1)}, u32[]{:S(2)}, u32[]{:S(2)}) collective-permute-start(f32[4,80,128]{2,1,0:T(8,128)S(1)} %shard_map.107.refs_0_.refs_4_), channel_id=1, source_target_pairs={{0,4},{4,0},{8,12},{12,8},{1,5},{5,1},{9,13},{13,9},{2,6},{6,2},{1... | collective-permute-start | bytes 491528 | tf_op jit(solution)/shard_map/ppermute | solution.py:18
  35.2 11.3 %collective-permute-start.24 = (f32[4,80,128]{2,1,0:T(8,128)S(1)}, f32[4,80,128]{2,1,0:T(8,128)S(1)}, u32[]{:S(2)}, u32[]{:S(2)}) collective-permute-start(f32[4,80,128]{2,1,0:T(8,128)S(1)} %collective-permute-done.23.refs_2_.refs_5_), channel_id=1, source_target_pairs={{0,4},{4,0},{8,12},{12,8},{1,5},{5,1},{9,13},{13,9},{2,6},{6,2},{1... | collective-permute-start | bytes 491528 | tf_op jit(solution)/shard_map/ppermute | solution.py:18
  35.2 11.3 %collective-permute-start.13 = (f32[256,128]{1,0:T(8,128)S(1)}, f32[256,128]{1,0:T(8,128)S(1)}, u32[]{:S(2)}, u32[]{:S(2)}) collective-permute-start(f32[256,128]{1,0:T(8,128)S(1)} %collective-permute-done.12), channel_id=1, source_target_pairs={{0,1},{1,0},{2,3},{3,2},{4,5},{5,4},{6,7},{7,6},{8,9},{9,8},{10,11... | collective-permute-start | bytes 393224 | tf_op jit(solution)/shard_map/ppermute | solution.py:18
  40.9 27.3 %collective-permute-start.5 = (f32[352,128]{1,0:T(8,128)S(1)}, f32[352,128]{1,0:T(8,128)S(1)}, u32[]{:S(2)}, u32[]{:S(2)}) collective-permute-start(f32[352,128]{1,0:T(8,128)S(1)} %get-tuple-element.48), channel_id=1, source_target_pairs={{0,1},{1,0},{2,3},{3,2},{4,5},{5,4},{6,7},{7,6},{8,9},{9,8},{10,11... | collective-permute-start | bytes 540680 | tf_op jit(solution)/shard_map/ppermute | solution.py:18
  42.4 25.9 %collective-permute-start.6 = (f32[352,128]{1,0:T(8,128)S(1)}, f32[352,128]{1,0:T(8,128)S(1)}, u32[]{:S(2)}, u32[]{:S(2)}) collective-permute-start(f32[352,128]{1,0:T(8,128)S(1)} %get-tuple-element.49), channel_id=1, source_target_pairs={{0,2},{1,3},{2,0},{3,1},{4,6},{5,7},{6,4},{7,5},{8,10},{9,11},{10,... | collective-permute-start | bytes 540680 | tf_op jit(solution)/shard_map/ppermute | solution.py:18
  42.4 25.9 %collective-permute-start.7 = (f32[352,128]{1,0:T(8,128)S(1)}, f32[352,128]{1,0:T(8,128)S(1)}, u32[]{:S(2)}, u32[]{:S(2)}) collective-permute-start(f32[352,128]{1,0:T(8,128)S(1)} %get-tuple-element.50), channel_id=1, source_target_pairs={{0,3},{1,2},{2,1},{3,0},{4,7},{5,6},{6,5},{7,4},{8,11},{9,10},{10,... | collective-permute-start | bytes 540680 | tf_op jit(solution)/shard_map/ppermute | solution.py:18
  46.4 21.8 %collective-permute-start.15 = (f32[256,128]{1,0:T(8,128)S(1)}, f32[256,128]{1,0:T(8,128)S(1)}, u32[]{:S(2)}, u32[]{:S(2)}) collective-permute-start(f32[256,128]{1,0:T(8,128)S(1)} %collective-permute-done.14), channel_id=1, source_target_pairs={{0,2},{1,3},{2,0},{3,1},{4,6},{5,7},{6,4},{7,5},{8,10},{9,11},{10,... | collective-permute-start | bytes 393224 | tf_op jit(solution)/shard_map/ppermute | solution.py:18
  46.4 21.8 %collective-permute-start.17 = (f32[256,128]{1,0:T(8,128)S(1)}, f32[256,128]{1,0:T(8,128)S(1)}, u32[]{:S(2)}, u32[]{:S(2)}) collective-permute-start(f32[256,128]{1,0:T(8,128)S(1)} %collective-permute-done.16), channel_id=1, source_target_pairs={{0,3},{1,2},{2,1},{3,0},{4,7},{5,6},{6,5},{7,4},{8,11},{9,10},{10,... | collective-permute-start | bytes 393224 | tf_op jit(solution)/shard_map/ppermute | solution.py:18
  69.9 10.3 %collective-permute-start.25 = (f32[576,128]{1,0:T(8,128)S(1)}, f32[576,128]{1,0:T(8,128)S(1)}, u32[]{:S(2)}, u32[]{:S(2)}) collective-permute-start(f32[576,128]{1,0:T(8,128)S(1)} %get-tuple-element.67.own), channel_id=1, source_target_pairs={{0,4},{4,0},{8,12},{12,8},{1,5},{5,1},{9,13},{13,9},{2,6},{6,2},{1... | collective-permute-start | bytes 884744 | tf_op jit(solution)/shard_map/ppermute | solution.py:18
  70.0 8.6 %collective-permute-start.32 = (f32[288,128]{1,0:T(8,128)S(1)}, f32[288,128]{1,0:T(8,128)S(1)}, u32[]{:S(2)}, u32[]{:S(2)}) collective-permute-start(f32[288,128]{1,0:T(8,128)S(1)} %get-tuple-element.76), channel_id=1, source_target_pairs={{0,3},{1,2},{2,1},{3,0},{4,7},{5,6},{6,5},{7,4},{8,11},{9,10},{10,... | collective-permute-start | bytes 442376 | tf_op jit(solution)/shard_map/ppermute | solution.py:18
  71.2 9.1 %collective-permute-start.27 = (f32[288,128]{1,0:T(8,128)S(1)}, f32[288,128]{1,0:T(8,128)S(1)}, u32[]{:S(2)}, u32[]{:S(2)}) collective-permute-start(f32[288,128]{1,0:T(8,128)S(1)} %get-tuple-element.71), channel_id=1, source_target_pairs={{0,1},{1,0},{2,3},{3,2},{4,5},{5,4},{6,7},{7,6},{8,9},{9,8},{10,11... | collective-permute-start | bytes 442376 | tf_op jit(solution)/shard_map/ppermute | solution.py:18
  80.6 7.5 %collective-permute-start.30 = (f32[256,128]{1,0:T(8,128)S(1)}, f32[256,128]{1,0:T(8,128)S(1)}, u32[]{:S(2)}, u32[]{:S(2)}) collective-permute-start(f32[256,128]{1,0:T(8,128)S(1)} %get-tuple-element.75), channel_id=1, source_target_pairs={{0,8},{4,12},{8,0},{12,4},{1,9},{5,13},{9,1},{13,5},{2,10},{6,14},... | collective-permute-start | bytes 393224 | tf_op jit(solution)/shard_map/ppermute | solution.py:18
  84.3 9.4 %collective-permute-start.29 = (f32[256,128]{1,0:T(8,128)S(1)}, f32[256,128]{1,0:T(8,128)S(1)}, u32[]{:S(2)}, u32[]{:S(2)}) collective-permute-start(f32[256,128]{1,0:T(8,128)S(1)} %get-tuple-element.73), channel_id=1, source_target_pairs={{0,8},{4,12},{8,0},{12,4},{1,9},{5,13},{9,1},{13,5},{2,10},{6,14},... | collective-permute-start | bytes 393224 | tf_op jit(solution)/shard_map/ppermute | solution.py:18
  86.4 9.9 %collective-permute-start.26 = (f32[256,128]{1,0:T(8,128)S(1)}, f32[256,128]{1,0:T(8,128)S(1)}, u32[]{:S(2)}, u32[]{:S(2)}) collective-permute-start(f32[256,128]{1,0:T(8,128)S(1)} %get-tuple-element.70), channel_id=1, source_target_pairs={{0,8},{4,12},{8,0},{12,4},{1,9},{5,13},{9,1},{13,5},{2,10},{6,14},... | collective-permute-start | bytes 393224 | tf_op jit(solution)/shard_map/ppermute | solution.py:18
  88.1 9.0 %collective-permute-start.31 = (f32[256,128]{1,0:T(8,128)S(1)}, f32[256,128]{1,0:T(8,128)S(1)}, u32[]{:S(2)}, u32[]{:S(2)}) collective-permute-start(f32[256,128]{1,0:T(8,128)S(1)} %add.25), channel_id=1, source_target_pairs={{0,2},{1,3},{2,0},{3,1},{4,6},{5,7},{6,4},{7,5},{8,10},{9,11},{10,... | collective-permute-start | bytes 393224 | tf_op jit(solution)/shard_map/ppermute | solution.py:18
  (25 other events, 150.8 us)
